TPU v7x, 256 devices: a whole 4x4x8 slice. The times are simulated.
256 devices in a mesh: row: 32 (over z, y_lo, core), col: 8 (over y_hi, x).
Axes of the slice: x: 4, y: 4 (y_hi: 2, y_lo: 2; y = y_hi * 2 + y_lo), z: 8, core: 2. Of those that a mesh axis runs over, the one named last changes fastest.
Arguments:
- queries: bfloat16 [256, 256, 2240], P('row', 'col'), may hold values from -6 to 6
- keys: bfloat16 [256, 256, 2240], P('row', 'col'), may hold values from -120 to 120
- values: bfloat16 [256, 256, 2240], P('row', 'col'), may hold values from -10 to 10
- features: bfloat16 [256, 256, 11200], P('row', 'col'), may hold values from -6 to 6
- conv_weight: bfloat16 [3, 3, 11200], replicated, may hold values from -2 to 2
- conv_bias: bfloat16 [11200], replicated, may hold values from -3 to 3
Outputs:
- attended: bfloat16 [256, 256, 2240], P('row', 'col')
- gated: bfloat16 [256, 256, 5600], P('row', 'col')
All inputs are finite; a program needn't handle non-finite values.
Results may differ from a plain program's by a relative error of at most 0.001.
Values may be sent and summed in bfloat16 or wider, within the bound.
A program may use at most 128 MiB of HBM per device.

v0:
```python
import jax
import jax.numpy as jnp
from jax import lax
from jax.sharding import PartitionSpec as P

HEADS = 70
HEAD_DIM = 32
HID = 5600


def padded_2(block, sides, width):
    for axis, dim in sides:
        count = lax.axis_size(axis)
        forward = [(i, i + 1) for i in range(count - 1)]
        backward = [(target, source) for source, target in forward]
        low = lax.ppermute(
            lax.slice_in_dim(block, block.shape[dim] - width, None, axis=dim), axis, forward
        )
        high = lax.ppermute(lax.slice_in_dim(block, 0, width, axis=dim), axis, backward)
        block = jnp.concatenate([low, block, high], axis=dim)
    return block


def on_device(queries, keys, values, features, conv_weight, conv_bias):
    tile_rows, tile_cols, channels = queries.shape
    key_heads = jnp.maximum(keys.reshape(-1, HEADS, HEAD_DIM), 0)
    value_heads = values.reshape(-1, HEADS, HEAD_DIM)
    local_state = jnp.einsum(
        "thj,thi->jhi", value_heads, key_heads, preferred_element_type=jnp.float32
    ).reshape(HEAD_DIM, channels)
    local_keys = jnp.sum(key_heads, axis=0, dtype=jnp.float32).reshape(1, channels)
    state_sum, key_sum = lax.psum((local_state, local_keys), ("row", "col"))
    kv_state = state_sum.reshape(HEAD_DIM, HEADS, HEAD_DIM)
    key_total = key_sum.reshape(HEADS, HEAD_DIM)
    query_heads = jnp.maximum(queries.reshape(-1, HEADS, HEAD_DIM), 0).astype(jnp.float32)
    numerator = jnp.einsum("thi,jhi->thj", query_heads, kv_state, precision=lax.Precision.HIGHEST)
    denominator = jnp.einsum("thi,hi->th", query_heads, key_total, precision=lax.Precision.HIGHEST)
    attended = (
        (numerator / (denominator[:, :, None] + 1e-15))
        .astype(jnp.bfloat16)
        .reshape(tile_rows, tile_cols, channels)
    )
    padded = padded_2(features, (("row", 0), ("col", 1)), 1)
    weight_float = conv_weight.astype(jnp.float32)
    conv_sum = conv_bias.astype(jnp.float32)
    for tap_row in range(3):
        for tap_col in range(3):
            window = padded[tap_row : tap_row + tile_rows, tap_col : tap_col + tile_cols]
            conv_sum = conv_sum + weight_float[tap_row, tap_col] * window.astype(jnp.float32)
    gated = (conv_sum[:, :, :HID] * jax.nn.silu(conv_sum[:, :, HID:])).astype(jnp.bfloat16)
    return (attended, gated)


def solution(mesh):
    return jax.shard_map(
        on_device,
        mesh=mesh,
        in_specs=(
            P("row", "col", None),
            P("row", "col", None),
            P("row", "col", None),
            P("row", "col", None),
            P(),
            P(),
        ),
        out_specs=(P("row", "col", None), P("row", "col", None)),
        check_vma=False,
    )
```

profile of v0, /device:TPU:1, one launch (start us, length us, event | category | flops | bytes accessed | tf_op | source)
XLA Modules:
  0.0 376.7 jit_solution(7483596677770068258)
XLA Ops:
  7.2 0.0 copy-start.6
  7.2 0.0 all-reduce.2.cloned.1.call-start
  7.2 2.4 fusion.13
  9.6 4.6 %collective-permute-start = (bf16[1,32,11200]{2,1,0:T(8,128)(2,1)S(1)}, bf16[1,32,11200]{2,1,0:T(8,128)(2,1)}, u32[]{:S(2)}, u32[]{:S(2)}) collective-permute-start(bf16[1,32,11200]{2,1,0:T(8,128)(2,1)S(1)} %get-tuple-element.14), channel_id=1, source_target_pairs={{0,8},{8,16},{16,24},{24,32},{32,40},{40,48},{48,56},{56,64},{64,7... | collective-permute-start | bytes 2150408 | tf_op jit(solution)/shard_map/ppermute | solution.py:16
  14.2 2.7 collective-permute-start.1
  16.9 1.4 broadcast_maximum_fusion.1
  18.2 5.0 %reshape.43 = bf16[256,70,32]{2,1,0:T(8,128)(2,1)} reshape(bf16[8,32,2240]{2,1,0:T(8,128)(2,1)S(1)} %broadcast_maximum_fusion.1) | data formatting | bytes 2293760 | tf_op jit(solution)/shard_map/max | solution.py:26
  23.3 0.0 copy-done.6
  23.3 4.9 %reshape.44 = bf16[256,70,32]{2,1,0:T(8,128)(2,1)} reshape(bf16[8,32,2240]{2,1,0:T(8,128)(2,1)S(1)} %copy-done.6) | data formatting | bytes 2293760 | tf_op jit(solution)/shard_map/reshape | solution.py:27
  28.2 6.3 %fusion.5 = f32[32,70,32]{0,2,1:T(8,128)} fusion(bf16[256,70,32]{2,1,0:T(8,128)(2,1)} %reshape.44, bf16[256,70,32]{2,1,0:T(8,128)(2,1)} %reshape.43), kind=kOutput, calls=%fused_computation.13 | convolution fusion | flops 36700160 | bytes 2580480 | tf_op jit(solution)/shard_map/thj,thi->jhi/dot_general | solution.py:28
  34.5 0.0 all-reduce.2.cloned.1.call-update
  34.6 0.0 copy-done.7
  34.6 1.0 fusion.14
  35.5 0.0 copy-done.5
  35.5 0.1 broadcast_maximum_fusion
  35.6 0.0 copy-start.15
  35.6 8.3 %copy.31 = bf16[8,32,11200]{2,0,1:T(8,128)(2,1)} copy(bf16[8,32,11200]{2,1,0:T(8,128)(2,1)} %param.9) | data formatting | bytes 11468800 | tf_op args[3]
  43.9 0.0 copy-done.15
  43.9 0.0 copy-start.2
  43.9 4.9 %reshape.45 = bf16[256,70,32]{2,1,0:T(8,128)(2,1)} reshape(bf16[8,32,2240]{2,1,0:T(8,128)(2,1)S(1)} %broadcast_maximum_fusion) | data formatting | bytes 2293760 | tf_op jit(solution)/shard_map/max | solution.py:35
  48.9 6.1 %copy.45 = bf16[256,70,32]{0,2,1:T(8,128)(2,1)S(1)} copy(bf16[256,70,32]{2,1,0:T(8,128)(2,1)} %reshape.45) | data formatting | bytes 2293760 | tf_op jit(solution)/shard_map/max | solution.py:35
  55.0 0.0 copy-done.2
  55.0 0.0 copy-start.3
  55.0 0.3 convert_reduce_fusion
  55.2 0.1 reshape.37
  55.3 80.7 %psum.15 = f32[70,32]{1,0:T(8,128)S(1)} all-reduce(f32[70,32]{1,0:T(8,128)S(1)} %reshape.37), channel_id=1, replica_groups=mesh['row'=32,'col'=8] {'row','col'}, use_global_device_ids=true, to_apply=%region_2.0 | all-reduce | flops 2240 | bytes 17920 | tf_op jit(solution)/shard_map/psum | solution.py:32
  136.0 0.6 fusion.11
  136.6 0.6 fusion.10
  137.3 0.0 copy-done.3
  137.3 0.0 collective-permute-done
  137.3 2.2 copy.30
  139.5 0.0 copy-start.4
  139.5 0.0 copy-start.14
  139.5 0.0 collective-permute-done.1
  139.5 2.3 copy.32
  141.9 0.0 copy-start
  141.9 1.1 copy-done
  143.0 2.1 pad_maximum_fusion.5
  145.1 2.1 collective-permute-start.2
  147.1 1.3 collective-permute-start.3
  148.4 146.6 %all-reduce.2.cloned.1.call-done = f32[32,70,32]{0,2,1:T(8,128)} async-done(((f32[32,70,32]{0,2,1:T(8,128)}), f32[32,70,32]{0,2,1:T(8,128)}) %all-reduce.2.cloned.1.call-update) | async-done | bytes 286736 | tf_op jit(solution)/shard_map/psum | solution.py:32
  295.0 0.0 copy-done.4
  295.0 0.0 copy-done.14
  295.0 3.4 fusion.4
  298.4 6.0 %reshape.38 = bf16[8,32,2240]{1,0,2:T(8,128)(2,1)} reshape(bf16[256,70,32]{0,2,1:T(8,128)(2,1)} %fusion.4) | data formatting | bytes 2293760 | tf_op jit(solution)/shard_map/reshape | solution.py:41
  304.5 6.3 %copy.38 = bf16[8,32,2240]{2,1,0:T(8,128)(2,1)} copy(bf16[8,32,2240]{1,0,2:T(8,128)(2,1)} %reshape.38) | data formatting | bytes 2293760
  310.8 0.0 copy-start.10
  310.8 0.0 copy-start.11
  310.8 0.0 copy-start.12
  310.9 0.0 copy-start.13
  310.9 0.0 collective-permute-done.2
  310.9 0.0 collective-permute-done.3
  310.9 22.1 %maximum_maximum_fusion = (bf16[10,33,11200]{2,0,1:T(8,128)(2,1)}, bf16[10,33,11200]{2,0,1:T(8,128)(2,1)}) fusion(bf16[1,32,11200]{2,0,1:T(2,128)(2,1)} %copy-done, bf16[8,32,11200]{2,0,1:T(8,128)(2,1)} %copy.31, bf16[1,32,11200]{2,0,1:T(2,128)(2,1)S(1)} %copy.30, bf16[10,1,11200]{2,0,1:T(8,128)(2,1)} %collective-permute-done.2, ...), kind=kLoop, calls=%fused_computation | loop fusion | flops 59136000 | bytes 22400000 | tf_op jit(solution)/shard_map/concatenate | solution.py:20
  333.0 0.0 slice-done
  333.0 0.0 slice-done.1
  333.0 0.0 copy-done.1
  333.0 0.0 copy-done.8
  333.0 0.0 copy-done.9
  333.0 0.0 copy-done.10
  333.0 0.0 copy-done.11
  333.1 0.0 copy-done.12
  333.1 29.1 %multiply_add_fusion = f32[8,32,11200]{2,0,1:T(8,128)} fusion(bf16[8,32,11200]{2,0,1:T(8,128)(2,1)S(1)} %bitcast.28, bf16[10,33,11200]{2,0,1:T(8,128)(2,1)} %get-tuple-element.11, bf16[1,32,11200]{2,0,1:T(2,128)(2,1)S(1)} %copy-done.1, bf16[10,33,11200]{2,0,1:T(8,128)(2,1)} %get-tuple-element.10, bf16[1,32,11200]{2,0,1:T(2,128)(2,1)S(1)} %copy.30, ...), kind=kLoop, calls=%fused_computation.2 | loop fusion | flops 94617600 | bytes 53491200 | tf_op jit(solution)/shard_map/add | solution.py:49
  362.2 5.2 %fusion = bf16[8,32,5600]{2,0,1:T(8,128)(2,1)S(1)} fusion(f32[8,32,11200]{2,0,1:T(8,128)} %multiply_add_fusion), kind=kLoop, calls=%fused_computation.4 | loop fusion | flops 8601600 | bytes 14336000 | tf_op jit(solution)/shard_map/convert_element_type | solution.py:50
  367.5 2.4 copy.39
  (10 shorter events, 0.0 us)
Async XLA Ops:
  7.2 16.1 %copy-start.6 = (bf16[8,32,2240]{2,1,0:T(8,128)(2,1)S(1)}, bf16[8,32,2240]{2,1,0:T(8,128)(2,1)}, u32[]{:S(2)}) copy-start(bf16[8,32,2240]{2,1,0:T(8,128)(2,1)} %param.8) | copy-start | bytes 3440644
  7.2 287.8 %all-reduce.2.cloned.1.call-start = ((), (), s32[]{:S(2)}) async-start(), calls=%async_computation | async-start | bytes 2293760 | tf_op jit(solution)/shard_map/psum | solution.py:32
  9.6 127.7 %collective-permute-start = (bf16[1,32,11200]{2,1,0:T(8,128)(2,1)S(1)}, bf16[1,32,11200]{2,1,0:T(8,128)(2,1)}, u32[]{:S(2)}, u32[]{:S(2)}) collective-permute-start(bf16[1,32,11200]{2,1,0:T(8,128)(2,1)S(1)} %get-tuple-element.14), channel_id=1, source_target_pairs={{0,8},{8,16},{16,24},{24,32},{32,40},{40,48},{48,56},{56,64},{64,7... | collective-permute-start | bytes 2150408 | tf_op jit(solution)/shard_map/ppermute | solution.py:16
  14.2 125.4 %collective-permute-start.1 = (bf16[1,32,11200]{2,1,0:T(8,128)(2,1)}, bf16[1,32,11200]{2,1,0:T(8,128)(2,1)}, u32[]{:S(2)}, u32[]{:S(2)}) collective-permute-start(bf16[1,32,11200]{2,1,0:T(8,128)(2,1)} %get-tuple-element.15), channel_id=1, source_target_pairs={{8,0},{16,8},{24,16},{32,24},{40,32},{48,40},{56,48},{64,56},{72,6... | collective-permute-start | bytes 2150408 | tf_op jit(solution)/shard_map/ppermute | solution.py:19
  28.2 6.4 %copy-start.7 = (bf16[3,3,11200]{2,1,0:T(4,128)(2,1)S(1)}, bf16[3,3,11200]{2,1,0:T(4,128)(2,1)}, u32[]{:S(2)}) copy-start(bf16[3,3,11200]{2,1,0:T(4,128)(2,1)} %param.10) | copy-start | bytes 604804
  28.2 7.3 %copy-start.5 = (bf16[8,32,2240]{2,1,0:T(8,128)(2,1)S(1)}, bf16[8,32,2240]{2,1,0:T(8,128)(2,1)}, u32[]{:S(2)}) copy-start(bf16[8,32,2240]{2,1,0:T(8,128)(2,1)} %param.6) | copy-start | bytes 3440644
  35.6 8.3 %copy-start.15 = (bf16[11200]{0:T(1024)(128)(2,1)S(1)}, bf16[11200]{0:T(1024)(128)(2,1)}, u32[]{:S(2)}) copy-start(bf16[11200]{0:T(1024)(128)(2,1)} %param.11) | copy-start | bytes 67204
  43.9 11.1 %copy-start.2 = (bf16[8,32,2240]{2,1,0:T(8,128)(2,1)S(1)}, bf16[8,32,2240]{2,1,0:T(8,128)(2,1)}, u32[]{:S(2)}) copy-start(bf16[8,32,2240]{2,1,0:T(8,128)(2,1)} %param.7) | copy-start | bytes 3440644
  55.0 82.3 %copy-start.3 = (bf16[256,70,32]{0,2,1:T(8,128)(2,1)}, bf16[256,70,32]{0,2,1:T(8,128)(2,1)S(1)}, u32[]{:S(2)}) copy-start(bf16[256,70,32]{0,2,1:T(8,128)(2,1)S(1)} %copy.45) | copy-start | bytes 3440644
  139.5 155.5 %copy-start.4 = (bf16[256,70,32]{0,2,1:T(8,128)(2,1)S(1)}, bf16[256,70,32]{0,2,1:T(8,128)(2,1)}, u32[]{:S(2)}) copy-start(bf16[256,70,32]{0,2,1:T(8,128)(2,1)} %copy-done.3) | copy-start | bytes 3440644
  139.5 155.5 %copy-start.14 = (f32[256,70]{0,1:T(8,128)S(1)}, f32[256,70]{0,1:T(8,128)}, u32[]{:S(2)}) copy-start(f32[256,70]{0,1:T(8,128)} %fusion.10) | copy-start | bytes 215044
  141.9 1.1 copy-start
  145.1 165.8 %collective-permute-start.2 = (bf16[10,1,11200]{2,0,1:T(8,128)(2,1)}, bf16[10,1,11200]{2,0,1:T(8,128)(2,1)}, u32[]{:S(2)}, u32[]{:S(2)}) collective-permute-start(bf16[10,1,11200]{2,0,1:T(8,128)(2,1)} %get-tuple-element.12), channel_id=1, source_target_pairs={{0,1},{1,2},{2,3},{3,4},{4,5},{5,6},{6,7},{8,9},{9,10},{10,11},{11... | collective-permute-start | bytes 672008 | tf_op jit(solution)/shard_map/ppermute | solution.py:16
  147.1 163.8 %collective-permute-start.3 = (bf16[10,1,11200]{2,0,1:T(8,128)(2,1)S(1)}, bf16[10,1,11200]{2,0,1:T(8,128)(2,1)}, u32[]{:S(2)}, u32[]{:S(2)}) collective-permute-start(bf16[10,1,11200]{2,0,1:T(8,128)(2,1)S(1)} %get-tuple-element.13), channel_id=1, source_target_pairs={{1,0},{2,1},{3,2},{4,3},{5,4},{6,5},{7,6},{9,8},{10,9},{11,10},{12... | collective-permute-start | bytes 672008 | tf_op jit(solution)/shard_map/ppermute | solution.py:19
  304.5 28.5 %slice-start = ((s8[5767168]{0:T(1024)(128)(4,1)}), s8[1572864]{0:T(1024)(128)(4,1)S(1)}, s32[]{:S(2)}) async-start(s8[5767168]{0:T(1024)(128)(4,1)} %bitcast.27), calls=%async_computation.1 | async-start | bytes 3145728
  310.8 22.2 %slice-start.1 = ((s8[5767168]{0:T(1024)(128)(4,1)}), s8[4194304]{0:T(1024)(128)(4,1)S(1)}, s32[]{:S(2)}) async-start(s8[5767168]{0:T(1024)(128)(4,1)} %bitcast.27), calls=%async_computation.2 | async-start | bytes 8388608
  310.8 22.2 %copy-start.1 = (bf16[1,32,11200]{2,0,1:T(2,128)(2,1)S(1)}, bf16[1,32,11200]{2,0,1:T(2,128)(2,1)}, u32[]{:S(2)}) copy-start(bf16[1,32,11200]{2,0,1:T(2,128)(2,1)} %copy-done) | copy-start | bytes 2150404
  310.8 22.2 %copy-start.8 = (f32[1,1,11200]{2,1,0:T(1,128)S(1)}, f32[1,1,11200]{2,1,0:T(1,128)}, u32[]{:S(2)}) copy-start(f32[1,1,11200]{2,1,0:T(1,128)} %get-tuple-element.19) | copy-start | bytes 134404
  310.8 22.2 %copy-start.9 = (f32[1,1,11200]{2,1,0:T(1,128)S(1)}, f32[1,1,11200]{2,1,0:T(1,128)}, u32[]{:S(2)}) copy-start(f32[1,1,11200]{2,1,0:T(1,128)} %get-tuple-element.20) | copy-start | bytes 134404
  310.8 22.2 %copy-start.10 = (f32[1,1,11200]{2,1,0:T(1,128)S(1)}, f32[1,1,11200]{2,1,0:T(1,128)}, u32[]{:S(2)}) copy-start(f32[1,1,11200]{2,1,0:T(1,128)} %get-tuple-element.21) | copy-start | bytes 134404
  310.8 22.2 %copy-start.11 = (f32[1,1,11200]{2,1,0:T(1,128)S(1)}, f32[1,1,11200]{2,1,0:T(1,128)}, u32[]{:S(2)}) copy-start(f32[1,1,11200]{2,1,0:T(1,128)} %get-tuple-element.22) | copy-start | bytes 134404
  310.8 22.2 %copy-start.12 = (f32[1,1,11200]{2,1,0:T(1,128)S(1)}, f32[1,1,11200]{2,1,0:T(1,128)}, u32[]{:S(2)}) copy-start(f32[1,1,11200]{2,1,0:T(1,128)} %get-tuple-element.23) | copy-start | bytes 134404
  310.9 22.2 %copy-start.13 = (f32[1,1,11200]{2,1,0:T(1,128)S(1)}, f32[1,1,11200]{2,1,0:T(1,128)}, u32[]{:S(2)}) copy-start(f32[1,1,11200]{2,1,0:T(1,128)} %get-tuple-element.24) | copy-start | bytes 134404
Sparse Core Ops, SparseCore 0:
  34.7 260.2 all-reduce.1
where the time goes:
time: 378 us; the launch traced here: 377 us
  waiting for transfers between devices  147 us (39%)
  blocking collectives  80.7 us (21%)
  other arithmetic  60.9 us (16%)
  local copies, waits for them, and re-layouts  53.2 us (14%)
  between operations  14.3 us (4%)
  starting transfers between devices  10.7 us (3%)
  matrix products  10.4 us (3%)
    psum x1, waiting for transfers between devices, on_device(): state_sum, key_sum = lax.psum((local_state, local_keys), ('row', 'col'))  147 us
    psum x1, blocking collectives, on_device(): state_sum, key_sum = lax.psum((local_state, local_keys), ('row', 'col'))  80.7 us
    add x1, other arithmetic, on_device(): conv_sum + weight_float[tap_row, tap_col] * window.astype(jnp.float32)  29.1 us
    concatenate x1, other arithmetic, padded_2(): block = jnp.concatenate([low, block, high], axis=dim)  22.1 us
    unnamed x39, local copies, waits for them, and re-layouts  18.2 us
    max x2, local copies, waits for them, and re-layouts, on_device(): jnp.maximum(queries.reshape(-1, HEADS, HEAD_DIM), 0).astype(jnp.float32)  11.1 us
  transfers between devices with their start and end apart: 5, of which 1 were waited for; matrix products, arithmetic and copies ran while one was open for 16% of the time, Pallas kernels for 0%

commit v1 on v0

v1 whole, which is shorter than its diff:
```python
import functools

import jax
import jax.numpy as jnp
from jax import lax
from jax.experimental import pallas as pl
from jax.experimental.pallas import tpu as pltpu
from jax.sharding import PartitionSpec as P

MESH = pl.DeviceIdType.MESH
F32 = jnp.float32
BF16 = jnp.bfloat16

HEAD_DIM = 32
HID = 5600
LANES = 128
BLOCKS = 18
TILES = 80
HALF = TILES // 2
QUARTER = HALF // 4
OWNERS = 5
SHARE = QUARTER // OWNERS
GATE_TILE = HID // LANES
GATE_SHIFT = LANES - HID % LANES


def iota(shape, dim):
    return lax.broadcasted_iota(jnp.int32, shape, dim)


def position():
    row, col = lax.axis_index("row"), lax.axis_index("col")
    core = lax.rem(row, 2)
    y = lax.div(col, 4) * 2 + lax.rem(lax.div(row, 2), 2)
    return row, col, core, lax.rem(col, 4), y, lax.div(row, 4)


def device(core, x, y, z):
    return (z * 4 + lax.rem(y, 2) * 2 + core, lax.div(y, 2) * 4 + x)


def mix_kernel(
    k_hbm, v_hbm, x_hbm, w_hbm, b_hbm,
    state_hbm, gated_hbm,
    kbuf, vbuf, xbuf, wbuf, bbuf, gbuf,
    up, down, left, right, send_left, send_right,
    corner_in, corner_out, prev, prev_edge,
    part, recv_core, recv_x, recv_z, recv_y, total,
    load_sem, store_sem, halo_send, halo_recv, edge_send, edge_recv, corner_send, corner_recv,
    core_send, core_recv, x_send, x_recv, z_send, z_recv, y_send, y_recv,
):
    row, col, core, x, y, z = position()
    rows, cols, channels = xbuf.shape
    n_row, n_col = lax.axis_size("row"), lax.axis_size("col")
    owner = z < OWNERS

    loads = [
        pltpu.make_async_copy(src, dst, load_sem.at[i])
        for i, (src, dst) in enumerate(
            [(x_hbm, xbuf), (k_hbm, kbuf), (v_hbm, vbuf), (w_hbm, wbuf), (b_hbm, bbuf)]
        )
    ]
    for load in loads:
        load.start()

    has_up, has_down = row > 0, row < n_row - 1
    has_left, has_right = col > 0, col < n_col - 1
    diagonals = [
        (0, has_up & has_left, -1, -1),
        (1, has_up & has_right, -1, 1),
        (2, has_down & has_left, 1, -1),
        (3, has_down & has_right, 1, 1),
    ]

    barrier = pltpu.get_barrier_semaphore()

    def greet(target):
        pl.semaphore_signal(barrier, inc=1, device_id=target, device_id_type=MESH)

    core_mate = device(1 - core, x, y, z)
    x_mates = [device(core, lax.rem(x + d, 4), y, z) for d in range(1, 4)]
    y_mates = [device(core, x, lax.rem(y + d, 4), z) for d in range(1, 4)]
    z_mates = [device(core, x, y, lax.rem(z + d, 8)) for d in range(1, 8)]
    for mate in [core_mate] + x_mates + y_mates + z_mates:
        greet(mate)
    sides = [(has_up, (row - 1, col)), (has_down, (row + 1, col)), (has_left, (row, col - 1)), (has_right, (row, col + 1))]
    for there, target in sides + [(t, (row + a, col + b)) for _, t, a, b in diagonals]:
        pl.when(there)(functools.partial(greet, target))

    @pl.when(row == 0)
    def _():
        up[...] = jnp.zeros_like(up)

    @pl.when(row == n_row - 1)
    def _():
        down[...] = jnp.zeros_like(down)

    @pl.when(col == 0)
    def _():
        left[...] = jnp.zeros_like(left)

    @pl.when(col == n_col - 1)
    def _():
        right[...] = jnp.zeros_like(right)

    for i, there, _, _ in diagonals:
        @pl.when(jnp.logical_not(there))
        def _():
            corner_in[i] = jnp.zeros_like(corner_in[i])

    one = jnp.int32(1)
    up_n, down_n = jnp.minimum(row, one), jnp.minimum(n_row - 1 - row, one)
    left_n, right_n = jnp.minimum(col, one), jnp.minimum(n_col - 1 - col, one)
    pl.semaphore_wait(barrier, 14 + (1 + up_n + down_n) * (1 + left_n + right_n) - 1)

    def remote(src, dst, send, recv, target):
        return pltpu.make_async_remote_copy(
            src_ref=src, dst_ref=dst, send_sem=send, recv_sem=recv, device_id=target, device_id_type=MESH
        )

    to_up = remote(x_hbm.at[0], down, halo_send.at[0], halo_recv.at[0], (row - 1, col))
    to_down = remote(x_hbm.at[rows - 1], up, halo_send.at[1], halo_recv.at[1], (row + 1, col))
    pl.when(has_up)(to_up.start)
    pl.when(has_down)(to_down.start)

    i8 = iota((8, LANES), 0)
    lane = iota((8, LANES), 1)

    loads[0].wait()

    def edge_tile(lanes, width):
        row_id = iota((8, width), 0)
        low = high = jnp.zeros((8, width), F32)
        for r in range(rows):
            first = xbuf[r, 0:16, lanes].astype(F32)[0:1]
            last = xbuf[r, cols - 16 : cols, lanes].astype(F32)[15:16]
            if r in (0, rows - 1):
                place = 0 if r == 0 else 2
                corner_out[place, :, lanes] = first
                corner_out[place + 1, :, lanes] = last
            low = jnp.where(row_id == r, first, low)
            high = jnp.where(row_id == r, last, high)
        send_left[:, lanes] = low.astype(BF16)
        send_right[:, lanes] = high.astype(BF16)

    full_tiles = channels // LANES
    tail = channels - full_tiles * LANES

    @pl.loop(0, full_tiles)
    def _(t):
        edge_tile(pl.ds(pl.multiple_of(t * LANES, LANES), LANES), LANES)

    edge_tile(slice(full_tiles * LANES, channels), tail)

    to_left = remote(send_left, right, edge_send.at[0], edge_recv.at[0], (row, col - 1))
    to_right = remote(send_right, left, edge_send.at[1], edge_recv.at[1], (row, col + 1))
    pl.when(has_left)(to_left.start)
    pl.when(has_right)(to_right.start)
    to_corner = [
        remote(corner_out.at[i], corner_in.at[3 - i], corner_send.at[i], corner_recv.at[3 - i], (row + a, col + b))
        for i, _, a, b in diagonals
    ]
    for i, there, _, _ in diagonals:
        pl.when(there)(to_corner[i].start)

    loads[1].wait()
    loads[2].wait()
    ones = jnp.ones((rows * cols, LANES), BF16)
    sums = [jnp.zeros((8, LANES), F32)] * 4
    for block in range(BLOCKS):
        start = block * LANES
        width = min(LANES, kbuf.shape[2] - start)
        keys = jnp.maximum(kbuf[:, :, start : start + width], 0).reshape(rows * cols, width)
        values = vbuf[:, :, start : start + width].reshape(rows * cols, width)
        contract = (((0,), (0,)), ((), ()))
        if width == LANES:
            both = lax.dot_general(
                keys, jnp.concatenate([values, ones], axis=1), contract, preferred_element_type=F32
            )
            state, key_sum = both[:, :LANES], both[:, LANES:]
        else:
            state = lax.dot_general(keys, values, contract, preferred_element_type=F32)
            state = jnp.concatenate([state, jnp.zeros((width, LANES - width), F32)], axis=1)
            key_sum = lax.dot_general(keys, ones, contract, preferred_element_type=F32)
        heads = width // HEAD_DIM
        for group in range(4):
            tile = jnp.zeros((8, LANES), F32)
            for h in range(heads):
                at = slice(h * HEAD_DIM + group * 8, h * HEAD_DIM + group * 8 + 8)
                tile = jnp.where(lax.div(lane, HEAD_DIM) == h, state[at], tile)
                sums[group] = jnp.where(lane == block * 4 + h, key_sum[at], sums[group])
            part[block * 4 + group] = tile
    for group in range(4):
        part[BLOCKS * 4 + group] = sums[group]
        part[BLOCKS * 4 + 4 + group] = jnp.zeros((8, LANES), F32)

    mine_core, mine_x = core * HALF, core * HALF + x * QUARTER
    mine_z = mine_x + z * SHARE
    add_core = remote(
        part.at[pl.ds((1 - core) * HALF, HALF)], recv_core, core_send.at[0], core_recv.at[0], core_mate
    )
    add_x = [
        remote(
            part.at[pl.ds(core * HALF + lax.rem(x + d, 4) * QUARTER, QUARTER)],
            recv_x.at[d - 1], x_send.at[d - 1], x_recv.at[d - 1], x_mates[d - 1],
        )
        for d in range(1, 4)
    ]

    def owned(d):
        return mine_x + jnp.minimum(lax.rem(z + d, 8), OWNERS - 1) * SHARE

    def owns(d):
        return lax.rem(z + d, 8) < OWNERS

    add_z = [
        remote(
            part.at[pl.ds(owned(d), SHARE)], recv_z.at[d - 1],
            z_send.at[d - 1], z_recv.at[d - 1], z_mates[d - 1],
        )
        for d in range(1, 8)
    ]
    own = pl.ds(owned(0), SHARE)
    add_y = [
        remote(part.at[own], recv_y.at[d - 1], y_send.at[d - 1], y_recv.at[d - 1], y_mates[d - 1])
        for d in range(1, 4)
    ]
    give_z = [
        remote(total.at[own], total.at[own], z_send.at[6 + d], z_recv.at[6 + d], z_mates[d - 1])
        for d in range(1, 8)
    ]
    get_z = [
        remote(
            total.at[pl.ds(owned(8 - d), SHARE)], total.at[pl.ds(owned(8 - d), SHARE)],
            z_send.at[6 + d], z_recv.at[6 + d], z_mates[d - 1],
        )
        for d in range(1, 8)
    ]
    all_x = pl.ds(mine_x, QUARTER)
    give_x = [
        remote(total.at[all_x], total.at[all_x], x_send.at[2 + d], x_recv.at[2 + d], x_mates[d - 1])
        for d in range(1, 4)
    ]
    get_x = [
        remote(
            total.at[pl.ds(core * HALF + lax.rem(x + 4 - d, 4) * QUARTER, QUARTER)],
            total.at[pl.ds(core * HALF + lax.rem(x + 4 - d, 4) * QUARTER, QUARTER)],
            x_send.at[2 + d], x_recv.at[2 + d], x_mates[d - 1],
        )
        for d in range(1, 4)
    ]
    all_core = pl.ds(mine_core, HALF)
    other_core = pl.ds((1 - core) * HALF, HALF)
    give_core = remote(total.at[all_core], total.at[all_core], core_send.at[1], core_recv.at[1], core_mate)
    get_core = remote(total.at[other_core], total.at[other_core], core_send.at[1], core_recv.at[1], core_mate)

    add_core.start()

    def sum_core():
        add_core.wait_recv()
        part[all_core] = part[all_core] + recv_core[...]
        for copy in add_x:
            copy.start()

    def sum_x():
        for copy in add_x:
            copy.wait_recv()
        part[all_x] = part[all_x] + recv_x[0] + recv_x[1] + recv_x[2]
        for d in range(1, 8):
            pl.when(owns(d))(add_z[d - 1].start)

    def sum_z():
        @pl.when(owner)
        def _():
            for copy in add_z:
                copy.wait_recv()
            got = part[own]
            for d in range(7):
                got = got + recv_z[d]
            part[own] = got
            for copy in add_y:
                copy.start()

    def sum_y():
        @pl.when(owner)
        def _():
            for copy in add_y:
                copy.wait_recv()
            total[own] = part[own] + recv_y[0] + recv_y[1] + recv_y[2]
            for copy in give_z:
                copy.start()

    def share_z():
        for d in range(1, 8):
            pl.when(owns(8 - d))(get_z[d - 1].wait_recv)
        for copy in give_x:
            copy.start()

    def share_x():
        for copy in get_x:
            copy.wait_recv()
        give_core.start()

    loads[3].wait()
    loads[4].wait()
    pl.when(has_right)(to_left.wait_recv)
    pl.when(has_left)(to_right.wait_recv)

    def conv(lanes, width, out_rows, fetch, low, high):
        weight = [wbuf[a, :, lanes].astype(F32) for a in range(3)]
        weight = [[weight[a][b : b + 1] for b in range(3)] for a in range(3)]
        bias = bbuf[:, lanes].astype(F32)
        sub = iota((8, width), 0)
        sources = {}
        for r in out_rows:
            for a in (-1, 0, 1):
                if r + a not in sources:
                    sources[r + a] = fetch(r + a)
        results = []
        for r in out_rows:
            around = [sources[r - 1], sources[r], sources[r + 1]]
            taps = []
            for b in range(3):
                taps.append(weight[0][b] * around[0] + weight[1][b] * around[1] + weight[2][b] * around[2])
            middle = taps[1] + bias
            groups = cols // 8
            from_low = [pltpu.roll(taps[0][8 * g : 8 * g + 8], 1, axis=0) for g in range(groups)]
            from_high = [pltpu.roll(taps[2][8 * g : 8 * g + 8], 7, axis=0) for g in range(groups)]
            low_edge = jnp.broadcast_to(
                sum(weight[a][0] * low(r + a - 1) for a in range(3)), (8, width))
            high_edge = jnp.broadcast_to(
                sum(weight[a][2] * high(r + a - 1) for a in range(3)), (8, width))
            out = []
            for g in range(groups):
                before = from_low[g - 1] if g else low_edge
                after = from_high[g + 1] if g + 1 < groups else high_edge
                out.append(
                    middle[8 * g : 8 * g + 8]
                    + jnp.where(sub == 0, before, from_low[g])
                    + jnp.where(sub == 7, after, from_high[g])
                )
            results.append(out)
        return results

    def silu(v):
        half = 0.5 * v
        return half + half * jnp.tanh(half)

    def sources_at(lanes):
        def fetch(r):
            if r < 0:
                return up[:, lanes].astype(F32)
            if r >= rows:
                return down[:, lanes].astype(F32)
            return xbuf[r, :, lanes].astype(F32)

        low_rows = left[:, lanes].astype(F32)
        high_rows = right[:, lanes].astype(F32)

        def low(r):
            if r < 0:
                return corner_in[0, :, lanes]
            return corner_in[2, :, lanes] if r >= rows else low_rows[r : r + 1]

        def high(r):
            if r < 0:
                return corner_in[1, :, lanes]
            return corner_in[3, :, lanes] if r >= rows else high_rows[r : r + 1]

        return fetch, low, high

    def gate_of(lanes, width, out_rows):
        turned = []
        for per_row in conv(lanes, width, out_rows, *sources_at(lanes)):
            for v in per_row:
                v = silu(v)
                if width < LANES:
                    v = jnp.concatenate([v, jnp.zeros((8, LANES - width), F32)], axis=1)
                turned.append(pltpu.roll(v, GATE_SHIFT, axis=1))
        return turned

    def gate_tile(u, out_rows, carry, last=False):
        start = u * LANES if last else pl.multiple_of(u * LANES, LANES)
        lanes = pl.ds(start, LANES)
        value = conv(lanes, LANES, out_rows, *sources_at(lanes))
        if last:
            gate_lanes, width = slice(full_tiles * LANES, channels), tail
        else:
            gate_lanes, width = pl.ds(pl.multiple_of((u + GATE_TILE + 1) * LANES, LANES), LANES), LANES
        turned = gate_of(gate_lanes, width, out_rows)
        for i, r in enumerate(out_rows):
            for pair in range(cols // 16):
                halves = []
                for g in (2 * pair, 2 * pair + 1):
                    at = i * (cols // 8) + g
                    gate = jnp.where(lane < GATE_SHIFT, carry[at], turned[at])
                    carry[at] = turned[at]
                    halves.append(value[i][g] * gate)
                out = jnp.concatenate(halves, axis=0).astype(BF16)
                if last:
                    gbuf[r, 16 * pair : 16 * pair + 16, u * LANES : HID] = out[:, : HID - u * LANES]
                else:
                    gbuf[r, 16 * pair : 16 * pair + 16, lanes] = out

    def all_tiles(out_rows, carry, steps):
        for at, v in enumerate(gate_of(slice(GATE_TILE * LANES, GATE_TILE * LANES + LANES), LANES, out_rows)):
            carry[at] = v

        @pl.loop(0, GATE_TILE)
        def _(u):
            gate_tile(u, out_rows, carry)
            for at, step in steps:
                pl.when(u == at)(step)

        gate_tile(GATE_TILE, out_rows, carry, last=True)

    inner = list(range(1, rows - 1))
    all_tiles(inner, prev, [(8, sum_core), (18, sum_x), (28, sum_z), (38, sum_y)])
    store_inner = pltpu.make_async_copy(
        gbuf.at[pl.ds(1, rows - 2)], gated_hbm.at[pl.ds(1, rows - 2)], store_sem.at[0]
    )
    store_inner.start()
    share_z()
    share_x()
    get_core.wait_recv()
    store_state = pltpu.make_async_copy(total, state_hbm, store_sem.at[1])
    store_state.start()

    pl.when(has_down)(to_up.wait_recv)
    pl.when(has_up)(to_down.wait_recv)
    for i, there, _, _ in diagonals:
        pl.when(there)(to_corner[3 - i].wait_recv)
    all_tiles([0, rows - 1], prev_edge, [])
    store_first = pltpu.make_async_copy(gbuf.at[0], gated_hbm.at[0], store_sem.at[2])
    store_last = pltpu.make_async_copy(gbuf.at[rows - 1], gated_hbm.at[rows - 1], store_sem.at[3])
    store_first.start()
    store_last.start()

    pl.when(has_up)(to_up.wait_send)
    pl.when(has_down)(to_down.wait_send)
    pl.when(has_left)(to_left.wait_send)
    pl.when(has_right)(to_right.wait_send)
    for i, there, _, _ in diagonals:
        pl.when(there)(to_corner[i].wait_send)
    for copy in [add_core, give_core] + add_x + give_x:
        copy.wait_send()
    for d in range(1, 8):
        pl.when(owns(d))(add_z[d - 1].wait_send)

    @pl.when(owner)
    def _():
        for copy in add_y + give_z:
            copy.wait_send()

    for store in [store_inner, store_state, store_first, store_last]:
        store.wait()


def mix(keys, values, features, conv_weight, conv_bias):
    rows, cols, channels = features.shape
    width = keys.shape[2]
    sem = pltpu.SemaphoreType.DMA
    tiles = lambda *lead: pltpu.VMEM(lead + (8, LANES), F32)
    anywhere = pl.BlockSpec(memory_space=pl.ANY)
    return pl.pallas_call(
        mix_kernel,
        name="mix",
        out_shape=(
            jax.ShapeDtypeStruct((TILES, 8, LANES), F32),
            jax.ShapeDtypeStruct((rows, cols, HID), BF16),
        ),
        in_specs=[anywhere] * 5,
        out_specs=[anywhere] * 2,
        scratch_shapes=[
            pltpu.VMEM((rows, cols, width), BF16),
            pltpu.VMEM((rows, cols, width), BF16),
            pltpu.VMEM((rows, cols, channels), BF16),
            pltpu.VMEM((3, 3, channels), BF16),
            pltpu.VMEM((1, channels), BF16),
            pltpu.VMEM((rows, cols, HID), BF16),
            pltpu.VMEM((cols, channels), BF16),
            pltpu.VMEM((cols, channels), BF16),
            pltpu.VMEM((rows, channels), BF16),
            pltpu.VMEM((rows, channels), BF16),
            pltpu.VMEM((rows, channels), BF16),
            pltpu.VMEM((rows, channels), BF16),
            pltpu.VMEM((4, 1, channels), F32),
            pltpu.VMEM((4, 1, channels), F32),
            tiles((rows - 2) * cols // 8),
            tiles(2 * cols // 8),
            tiles(TILES),
            tiles(HALF),
            tiles(3, QUARTER),
            tiles(7, SHARE),
            tiles(3, SHARE),
            tiles(TILES),
            sem((5,)), sem((4,)), sem((2,)), sem((2,)), sem((2,)), sem((2,)), sem((4,)), sem((4,)),
            sem((2,)), sem((2,)), sem((6,)), sem((6,)), sem((14,)), sem((14,)), sem((3,)), sem((3,)),
        ],
        compiler_params=pltpu.CompilerParams(
            collective_id=0, has_side_effects=True, vmem_limit_bytes=48 << 20
        ),
        cost_estimate=pl.CostEstimate(flops=100_000_000, bytes_accessed=12_000_000, transcendentals=1_500_000),
    )(keys, values, features, conv_weight, conv_bias.reshape(1, channels))


def attend_kernel(q_hbm, state, mixed_hbm, attended_hbm, gated_hbm, qbuf, abuf, matrix, sem):
    rows, cols, width = qbuf.shape
    move = pltpu.make_async_copy(mixed_hbm, gated_hbm, sem.at[0])
    load = pltpu.make_async_copy(q_hbm, qbuf, sem.at[1])
    load.start()
    move.start()

    lane = iota((HEAD_DIM, LANES), 1)
    head_of_lane = lax.div(lane, HEAD_DIM)

    def split(v):
        high = v.astype(BF16)
        return high, (v - high.astype(F32)).astype(BF16)

    sum_high, sum_low = split(state[pl.ds(BLOCKS * 4, 4)].reshape(HEAD_DIM, LANES))

    def block_diagonal(v):
        v = v.astype(F32)
        return jnp.concatenate([jnp.where(head_of_lane == h, v, 0.0) for h in range(4)], axis=0).astype(BF16)

    def build(block):
        high, low = split(state[pl.ds(block * 4, 4)].reshape(HEAD_DIM, LANES))
        picks = (iota((LANES, LANES), 0) == block * 4 + lax.div(iota((LANES, LANES), 1), HEAD_DIM))
        picks = picks.astype(F32).astype(BF16)
        key_high = jnp.dot(sum_high, picks, preferred_element_type=F32)
        key_low = jnp.dot(sum_low, picks, preferred_element_type=F32)
        top = jnp.concatenate([block_diagonal(high), block_diagonal(key_high)], axis=1)
        bottom = jnp.concatenate([block_diagonal(low), block_diagonal(key_low)], axis=1)
        matrix[block] = jnp.concatenate([top, bottom], axis=0)

    for block in range(BLOCKS):
        build(block)
    load.wait()
    for block in range(BLOCKS):
        start = block * LANES
        size = min(LANES, width - start)
        queries = jnp.maximum(qbuf[:, :, start : start + size], 0).reshape(rows * cols, size)
        if size < LANES:
            queries = jnp.concatenate([queries, jnp.zeros((rows * cols, LANES - size), BF16)], axis=1)
        both = jnp.dot(jnp.concatenate([queries, queries], axis=1), matrix[block], preferred_element_type=F32)
        out = (both[:, :LANES] / (both[:, LANES:] + 1e-15)).astype(BF16).reshape(rows, cols, LANES)
        abuf[:, :, start : start + size] = out[:, :, :size]
    store = pltpu.make_async_copy(abuf, attended_hbm, sem.at[2])
    store.start()
    store.wait()
    move.wait()


def attend(queries, state, mixed):
    anywhere = pl.BlockSpec(memory_space=pl.ANY)
    return pl.pallas_call(
        attend_kernel,
        name="attend",
        out_shape=(
            jax.ShapeDtypeStruct(queries.shape, BF16),
            jax.ShapeDtypeStruct(mixed.shape, BF16),
        ),
        in_specs=[anywhere, pl.BlockSpec(memory_space=pltpu.VMEM), anywhere],
        out_specs=[anywhere] * 2,
        scratch_shapes=[
            pltpu.VMEM(queries.shape, BF16),
            pltpu.VMEM(queries.shape, BF16),
            pltpu.VMEM((BLOCKS, 2 * LANES, 2 * LANES), BF16),
            pltpu.SemaphoreType.DMA((3,)),
        ],
        compiler_params=pltpu.CompilerParams(vmem_limit_bytes=32 << 20),
        cost_estimate=pl.CostEstimate(flops=600_000_000, bytes_accessed=8_000_000, transcendentals=0),
    )(queries, state, mixed)


def on_device(queries, keys, values, features, conv_weight, conv_bias):
    state, mixed = mix(keys, values, features, conv_weight, conv_bias)
    return attend(queries, state, mixed)


def solution(mesh):
    return jax.shard_map(
        on_device,
        mesh=mesh,
        in_specs=(
            P("row", "col", None),
            P("row", "col", None),
            P("row", "col", None),
            P("row", "col", None),
            P(),
            P(),
        ),
        out_specs=(P("row", "col", None), P("row", "col", None)),
        check_vma=False,
    )
```

time: 378 us -> 62 us (0.16)
  waiting for transfers between devices: 147 us -> 0 us
  blocking collectives: 80.7 us -> 0 us
  other arithmetic: 60.9 us -> 0 us
  Pallas kernels: 0 us -> 56.8 us
  local copies, waits for them, and re-layouts: 53.2 us -> 4.25 us
  between operations: 14.3 us -> 0.66 us
  starting transfers between devices: 10.7 us -> 0 us
  matrix products: 10.4 us -> 0 us
    psum x1 -> x0, waiting for transfers between devices: 147 us -> none  [on_device(): state_sum, key_sum = lax.psum((local_state, local_keys), ('row', 'col'))]
    psum x1 -> x0, blocking collectives: 80.7 us -> none  [on_device(): state_sum, key_sum = lax.psum((local_state, local_keys), ('row', 'col'))]
    pallas_call x0 -> x2, Pallas kernels: none -> 56.8 us  [the longest x1 54.5 us: mix(): pl.pallas_call(mix_kernel, name='mix', out_shape=(jax.ShapeDtypeStruct((T...]
    add x2 -> x0, other arithmetic: 29.8 us -> none  [the longest x1 29.1 us: on_device(): conv_sum + weight_float[tap_row, tap_col] * window.astype(jnp.float32)]
    concatenate x1 -> x0, other arithmetic: 22.1 us -> none  [padded_2(): block = jnp.concatenate([low, block, high], axis=dim)]
    max x3 -> x0, local copies, waits for them, and re-layouts: 16.1 us -> none  [the longest x2 11.1 us: on_device(): jnp.maximum(queries.reshape(-1, HEADS, HEAD_DIM), 0).astype(jnp.float32)]
    unnamed x39 -> x8, local copies, waits for them, and re-layouts: 18.2 us -> 3.49 us
    ppermute x4 -> x0, starting transfers between devices: 10.6 us -> none  [the longest x2 6.64 us: padded_2(): lax.ppermute(lax.slice_in_dim(block, block.shape[dim] - width, None, axis...]
  transfers between devices with their start and end apart: 5 -> 0, of which waited for: 1 -> 0; matrix products, arithmetic and copies ran while one was open for 16% -> 0% of each run, Pallas kernels for 0% -> 0%
where the time goes in v1:
time: 62 us; the launch traced here: 61.8 us
  Pallas kernels  56.8 us (92%)
  local copies, waits for them, and re-layouts  4.25 us (7%)
  between operations  0.66 us (1%)
    pallas_call x1, Pallas kernels, mix(): pl.pallas_call(mix_kernel, name='mix', out_shape=(jax.ShapeDtypeStruct((T...  54.5 us
    unnamed x8, local copies, waits for them, and re-layouts  3.49 us
    pallas_call x1, Pallas kernels, attend(): pl.pallas_call(attend_kernel, name='attend', out_shape=(jax.ShapeDtypeStr...  2.32 us

profile of v1, /device:TPU:1, one launch (start us, length us, event | category | flops | bytes accessed | tf_op | source)
XLA Modules:
  0.0 61.8 jit_solution(7733236285919116740)
XLA Ops:
  0.6 0.8 %reshape.7.b_hbm = bf16[1,11200]{1,0:T(2,128)(2,1)S(1)} reshape(bf16[11200]{0:T(1024)(128)(2,1)} %param.11) | data formatting | bytes 44800 | tf_op jit(solution)/shard_map/reshape | solution.py:504
  1.4 0.0 copy-start
  1.4 1.3 %copy-done = bf16[8,32,2240]{2,1,0:T(8,128)(2,1)S(1)} copy-done((bf16[8,32,2240]{2,1,0:T(8,128)(2,1)S(1)}, bf16[8,32,2240]{2,1,0:T(8,128)(2,1)}, u32[]{:S(2)}) %copy-start) | copy-done | bytes 1146904
  2.7 0.0 copy-start.1
  2.7 1.3 %copy-done.1 = bf16[8,32,2240]{2,1,0:T(8,128)(2,1)S(1)} copy-done((bf16[8,32,2240]{2,1,0:T(8,128)(2,1)S(1)}, bf16[8,32,2240]{2,1,0:T(8,128)(2,1)}, u32[]{:S(2)}) %copy-start.1) | copy-done | bytes 1146904
  3.9 0.0 copy-start.3
  3.9 1.0 %copy-done.3 = bf16[3,3,11200]{2,1,0:T(4,128)(2,1)S(1)} copy-done((bf16[3,3,11200]{2,1,0:T(4,128)(2,1)S(1)}, bf16[3,3,11200]{2,1,0:T(4,128)(2,1)}, u32[]{:S(2)}) %copy-start.3) | copy-done | bytes 201624
  4.9 0.0 copy-start.2
  4.9 54.5 %mix.1 = (f32[80,8,128]{2,1,0:T(8,128)S(1)}, bf16[8,32,5600]{2,1,0:T(8,128)(2,1)S(1)}) custom-call(bf16[8,32,2240]{2,1,0:T(8,128)(2,1)S(1)} %copy-done, bf16[8,32,2240]{2,1,0:T(8,128)(2,1)S(1)} %copy-done.1, bf16[8,32,11200]{2,1,0:T(8,128)(2,1)} %x_hbm.1, bf16[3,3,11200]{2,1,0:T(4,128)(2,1)S(1)} %copy-done.3, bf16[1,11200]{1,0:T(2,128)(2,1)S(1)} %reshape.7.b_hbm), custom_call_target="tpu_custom_call" | custom-call | flops 100000000 | bytes 12000000 | tf_op jit(solution)/shard_map/mix/pallas_call | solution.py:465
  59.4 0.0 copy-done.2
  59.4 2.3 %attend.1 = (bf16[8,32,2240]{2,1,0:T(8,128)(2,1)}, bf16[8,32,5600]{2,1,0:T(8,128)(2,1)}) custom-call(bf16[8,32,2240]{2,1,0:T(8,128)(2,1)S(1)} %copy-done.2, f32[80,8,128]{2,1,0:T(8,128)S(1)} %get-tuple-element.4.state, bf16[8,32,5600]{2,1,0:T(8,128)(2,1)S(1)} %get-tuple-element.5.mixed_hbm), custom_call_target="tpu_custom_call" | custom-call | flops 600000000 | bytes 8000000 | tf_op jit(solution)/shard_map/attend/pallas_call | solution.py:557
Async XLA Ops:
  1.4 1.3 %copy-start = (bf16[8,32,2240]{2,1,0:T(8,128)(2,1)S(1)}, bf16[8,32,2240]{2,1,0:T(8,128)(2,1)}, u32[]{:S(2)}) copy-start(bf16[8,32,2240]{2,1,0:T(8,128)(2,1)} %k_hbm.1) | copy-start | bytes 3440644
  2.7 1.3 %copy-start.1 = (bf16[8,32,2240]{2,1,0:T(8,128)(2,1)S(1)}, bf16[8,32,2240]{2,1,0:T(8,128)(2,1)}, u32[]{:S(2)}) copy-start(bf16[8,32,2240]{2,1,0:T(8,128)(2,1)} %v_hbm.1) | copy-start | bytes 3440644
  3.9 1.0 %copy-start.3 = (bf16[3,3,11200]{2,1,0:T(4,128)(2,1)S(1)}, bf16[3,3,11200]{2,1,0:T(4,128)(2,1)}, u32[]{:S(2)}) copy-start(bf16[3,3,11200]{2,1,0:T(4,128)(2,1)} %w_hbm.1) | copy-start | bytes 604804
  4.9 54.5 %copy-start.2 = (bf16[8,32,2240]{2,1,0:T(8,128)(2,1)S(1)}, bf16[8,32,2240]{2,1,0:T(8,128)(2,1)}, u32[]{:S(2)}) copy-start(bf16[8,32,2240]{2,1,0:T(8,128)(2,1)} %q_hbm.1) | copy-start | bytes 3440644

commit v2 on v0

v2 whole, which is shorter than its diff:
```python
import functools

import jax
import jax.numpy as jnp
from jax import lax
from jax.experimental import pallas as pl
from jax.experimental.pallas import tpu as pltpu
from jax.sharding import PartitionSpec as P

MESH = pl.DeviceIdType.MESH
F32 = jnp.float32
BF16 = jnp.bfloat16

HEAD_DIM = 32
HID = 5600
LANES = 128
BLOCKS = 18
USED = 10
QUARTER = 12
SHARE = QUARTER // 4
HALF = 4 * QUARTER
TILES = 2 * HALF
GATE_TILE = HID // LANES
GATE_SHIFT = LANES - HID % LANES
CHUNK = 4
CHUNKS = 11
DEPTH = 2
STEP_AT = (4, 18, 28, 41)


def slot(tile):
    return tile // USED * QUARTER + tile % USED


def iota(shape, dim):
    return lax.broadcasted_iota(jnp.int32, shape, dim)


def position():
    row, col = lax.axis_index("row"), lax.axis_index("col")
    core = lax.rem(row, 2)
    y = lax.div(col, 4) * 2 + lax.rem(lax.div(row, 2), 2)
    return row, col, core, lax.rem(col, 4), y, lax.div(row, 4)


def device(core, x, y, z):
    return (z * 4 + lax.rem(y, 2) * 2 + core, lax.div(y, 2) * 4 + x)


def mix_kernel(
    k_hbm, v_hbm, x_hbm, w_hbm, b_hbm,
    state_hbm, gated_hbm,
    kbuf, vbuf, xbuf, wbuf, bbuf, gbuf,
    halo, left, right, send_left, send_right,
    corner_in, corner_out, tail_in, tail_out, prev, gates,
    part, recv_core, recv_x, recv_z, recv_y, total,
    load_sem, store_sem, halo_send, halo_recv, mate_send, mate_recv, edge_send, edge_recv, corner_send, corner_recv,
    core_send, core_recv, x_send, x_recv, z_send, z_recv, y_send, y_recv,
):
    row, col, core, x, y, z = position()
    rows, cols, channels = xbuf.shape
    n_row, n_col = lax.axis_size("row"), lax.axis_size("col")

    loads = [
        pltpu.make_async_copy(src, dst, load_sem.at[i])
        for i, (src, dst) in enumerate(
            [(k_hbm, kbuf), (v_hbm, vbuf), (x_hbm, xbuf), (w_hbm, wbuf), (b_hbm, bbuf)]
        )
    ]
    for load in loads:
        load.start()

    has_up, has_down = row > 0, row < n_row - 1
    has_left, has_right = col > 0, col < n_col - 1
    diagonals = [
        (0, has_up & has_left, -1, -1),
        (1, has_up & has_right, -1, 1),
        (2, has_down & has_left, 1, -1),
        (3, has_down & has_right, 1, 1),
    ]

    barrier = pltpu.get_barrier_semaphore()

    def greet(target):
        pl.semaphore_signal(barrier, inc=1, device_id=target, device_id_type=MESH)

    core_mate = device(1 - core, x, y, z)
    x_mates = [device(core, lax.rem(x + d, 4), y, z) for d in range(1, 4)]
    y_mates = [device(core, x, lax.rem(y + d, 4), z) for d in range(1, 4)]
    z_mates = [device(core, x, y, lax.rem(z + d, 8)) for d in range(1, 8)]
    for mate in [core_mate] + x_mates + y_mates + z_mates:
        greet(mate)
    sides = [(has_up, (row - 1, col)), (has_down, (row + 1, col)), (has_left, (row, col - 1)), (has_right, (row, col + 1))]
    for there, target in sides + [(t, (row + a, col + b)) for _, t, a, b in diagonals]:
        pl.when(there)(functools.partial(greet, target))

    crosses = (row + core > 0) & (row + core < n_row)

    @pl.when(jnp.logical_not(crosses))
    def _():
        halo[core] = jnp.zeros_like(halo[core])

    @pl.when(col == 0)
    def _():
        left[...] = jnp.zeros_like(left)

    @pl.when(col == n_col - 1)
    def _():
        right[...] = jnp.zeros_like(right)

    for i, there, _, _ in diagonals:
        @pl.when(jnp.logical_not(there))
        def _():
            corner_in[i] = jnp.zeros_like(corner_in[i])

    one = jnp.int32(1)
    up_n, down_n = jnp.minimum(row, one), jnp.minimum(n_row - 1 - row, one)
    left_n, right_n = jnp.minimum(col, one), jnp.minimum(n_col - 1 - col, one)
    pl.semaphore_wait(barrier, 14 + (1 + up_n + down_n) * (1 + left_n + right_n) - 1)

    def remote(src, dst, send, recv, target):
        return pltpu.make_async_remote_copy(
            src_ref=src, dst_ref=dst, send_sem=send, recv_sem=recv, device_id=target, device_id_type=MESH
        )

    full_tiles = channels // LANES
    tail = channels - full_tiles * LANES
    mate_row = remote(x_hbm.at[(1 - core) * (rows - 1)], halo.at[core], mate_send.at[0], mate_recv.at[0], core_mate)
    far_row = x_hbm.at[core * (rows - 1)]
    far_target = (row + 2 * core - 1, col)
    mate_row.start()

    def chunk(at):
        copies = []
        for part_of in range(2):
            first, count = at * CHUNK + part_of * (GATE_TILE + 1), CHUNK
            if isinstance(at, int):
                count = min(CHUNK, full_tiles - first)
            lanes = pl.ds(pl.multiple_of(first * LANES, LANES), count * LANES)
            copies.append(remote(
                far_row.at[:, lanes], halo.at[1 - core, :, lanes],
                halo_send.at[part_of, at], halo_recv.at[part_of, at], far_target,
            ))
        return copies

    def start_chunk(at):
        @pl.when(crosses)
        def _():
            for copy in chunk(at):
                copy.start()

    def sent_chunk(at):
        @pl.when(crosses)
        def _():
            for copy in chunk(at):
                copy.wait_send()

    def received_chunk(at):
        @pl.when(crosses)
        def _():
            for copy in chunk(at):
                copy.wait_recv()

    def advance(step):
        if step >= DEPTH:
            sent_chunk(order[step - DEPTH])
        if step < CHUNKS:
            start_chunk(order[step])

    order = [CHUNKS - 1] + list(range(CHUNKS - 1))
    advance(0)

    lane = iota((8, LANES), 1)

    loads[0].wait()
    loads[1].wait()
    ones = jnp.ones((rows * cols, LANES), BF16)
    sums = [jnp.zeros((8, LANES), F32)] * 4
    for block in range(BLOCKS):
        start = block * LANES
        width = min(LANES, kbuf.shape[2] - start)
        keys = jnp.maximum(kbuf[:, :, start : start + width], 0).reshape(rows * cols, width)
        values = vbuf[:, :, start : start + width].reshape(rows * cols, width)
        contract = (((0,), (0,)), ((), ()))
        if width == LANES:
            both = lax.dot_general(
                keys, jnp.concatenate([values, ones], axis=1), contract, preferred_element_type=F32
            )
            state, key_sum = both[:, :LANES], both[:, LANES:]
        else:
            state = lax.dot_general(keys, values, contract, preferred_element_type=F32)
            state = jnp.concatenate([state, jnp.zeros((width, LANES - width), F32)], axis=1)
            key_sum = lax.dot_general(keys, ones, contract, preferred_element_type=F32)
        heads = width // HEAD_DIM
        for group in range(4):
            tile = jnp.zeros((8, LANES), F32)
            for h in range(heads):
                at = slice(h * HEAD_DIM + group * 8, h * HEAD_DIM + group * 8 + 8)
                tile = jnp.where(lax.div(lane, HEAD_DIM) == h, state[at], tile)
                sums[group] = jnp.where(lane == block * 4 + h, key_sum[at], sums[group])
            part[slot(block * 4 + group)] = tile
    for group in range(4):
        part[slot(BLOCKS * 4 + group)] = sums[group]
        part[slot(BLOCKS * 4 + 4 + group)] = jnp.zeros((8, LANES), F32)
    for quarter in range(8):
        for unused in range(USED, QUARTER):
            part[quarter * QUARTER + unused] = jnp.zeros((8, LANES), F32)

    def quarter(at, size=USED):
        return pl.ds(core * HALF + at * QUARTER, size)

    def share(at):
        return pl.ds(core * HALF + x * QUARTER + at * SHARE, SHARE)

    def ring(at, d, n):
        return lax.rem(at + d + n, n)

    mine_half, other_half = pl.ds(core * HALF, HALF), pl.ds((1 - core) * HALF, HALF)
    mine_x, mine_y = quarter(x), share(y)
    add_core = remote(part.at[other_half], recv_core, core_send.at[0], core_recv.at[0], core_mate)
    add_x, add_y, add_z, give_x, give_y, get_x, get_y = [], [], [], [], [], [], []
    for d in range(1, 4):
        a, b = d - 1, d + 2
        add_x.append(remote(part.at[quarter(ring(x, d, 4))], recv_x.at[a], x_send.at[a], x_recv.at[a], x_mates[a]))
        add_y.append(remote(part.at[share(ring(y, d, 4))], recv_y.at[a], y_send.at[a], y_recv.at[a], y_mates[a]))
        give_x.append(remote(total.at[mine_x], total.at[mine_x], x_send.at[b], x_recv.at[b], x_mates[a]))
        give_y.append(remote(total.at[mine_y], total.at[mine_y], y_send.at[b], y_recv.at[b], y_mates[a]))
        from_x, from_y = quarter(ring(x, -d, 4)), share(ring(y, -d, 4))
        get_x.append(remote(total.at[from_x], total.at[from_x], x_send.at[b], x_recv.at[b], x_mates[a]))
        get_y.append(remote(total.at[from_y], total.at[from_y], y_send.at[b], y_recv.at[b], y_mates[a]))
    for d in range(1, 8):
        add_z.append(remote(part.at[mine_y], recv_z.at[d - 1], z_send.at[d - 1], z_recv.at[d - 1], z_mates[d - 1]))
    give_core = remote(total.at[mine_half], total.at[mine_half], core_send.at[1], core_recv.at[1], core_mate)
    get_core = remote(total.at[other_half], total.at[other_half], core_send.at[1], core_recv.at[1], core_mate)

    def start_all(copies):
        for copy in copies:
            copy.start()

    def receive_all(copies):
        for copy in copies:
            copy.wait_recv()

    def sum_core():
        add_core.wait_recv()
        part[mine_half] = part[mine_half] + recv_core[...]
        start_all(add_x)

    def sum_x():
        receive_all(add_x)
        part[mine_x] = part[mine_x] + recv_x[0] + recv_x[1] + recv_x[2]
        start_all(add_y)

    def sum_y():
        receive_all(add_y)
        part[mine_y] = part[mine_y] + recv_y[0] + recv_y[1] + recv_y[2]
        start_all(add_z)

    def sum_z():
        receive_all(add_z)
        got = part[mine_y]
        for d in range(7):
            got = got + recv_z[d]
        total[mine_y] = got
        start_all(give_y)

    def share_y():
        receive_all(get_y)
        start_all(give_x)

    def share_x():
        receive_all(get_x)
        give_core.start()

    add_core.start()

    loads[2].wait()

    def edge_tile(lanes, width):
        row_id = iota((8, width), 0)
        low = high = jnp.zeros((8, width), F32)
        for r in range(rows):
            first = xbuf[r, 0:16, lanes].astype(F32)[0:1]
            last = xbuf[r, cols - 16 : cols, lanes].astype(F32)[15:16]
            if r in (0, rows - 1):
                place = 0 if r == 0 else 2
                corner_out[place, :, lanes] = first
                corner_out[place + 1, :, lanes] = last
            low = jnp.where(row_id == r, first, low)
            high = jnp.where(row_id == r, last, high)
        send_left[:, lanes] = low.astype(BF16)
        send_right[:, lanes] = high.astype(BF16)

    @pl.loop(0, full_tiles)
    def _(t):
        edge_tile(pl.ds(pl.multiple_of(t * LANES, LANES), LANES), LANES)

    edge_tile(slice(full_tiles * LANES, channels), tail)
    sum_core()
    rest = xbuf[core * (rows - 1), :, full_tiles * LANES :]
    tail_out[...] = jnp.concatenate([rest, jnp.zeros((cols, LANES - tail), BF16)], axis=1)
    far_tail = remote(tail_out, tail_in, mate_send.at[1], mate_recv.at[1], far_target)

    to_left = remote(send_left, right, edge_send.at[0], edge_recv.at[0], (row, col - 1))
    to_right = remote(send_right, left, edge_send.at[1], edge_recv.at[1], (row, col + 1))
    pl.when(has_left)(to_left.start)
    pl.when(has_right)(to_right.start)
    to_corner = [
        remote(corner_out.at[i], corner_in.at[3 - i], corner_send.at[i], corner_recv.at[3 - i], (row + a, col + b))
        for i, _, a, b in diagonals
    ]
    for i, there, _, _ in diagonals:
        pl.when(there)(to_corner[i].start)

    def bias_at(lanes, width):
        return bbuf[:, lanes].astype(F32)

    pl.when(crosses)(far_tail.start)
    advance(1)

    groups = cols // 8

    def conv(lanes, width, out_rows):
        sub = iota((8, width), 0)

        def wide(v):
            return jnp.broadcast_to(v, (8, width))

        weight = []
        for a in range(3):
            taps = wbuf[a, :, lanes].astype(F32)
            weight.append([wide(taps[b : b + 1]) for b in range(3)])
        bias = wide(bias_at(lanes, width))

        def fetch(r):
            source = []
            for at in range(0, cols, 16):
                if r < 0 or r >= rows:
                    pair = halo[int(r >= rows), at : at + 16, lanes]
                else:
                    pair = xbuf[r, at : at + 16, lanes]
                pair = pair.astype(F32)
                source += [pair[:8], pair[8:]]
            return source

        def edge(column, tap, corners):
            middle = column[:, lanes].astype(F32)
            above, below = pltpu.roll(middle, 1, axis=0), pltpu.roll(middle, 7, axis=0)
            if out_rows[0] == 0:
                above = jnp.where(sub == 0, wide(corner_in[corners[0], :, lanes]), above)
                below = jnp.where(sub == 7, wide(corner_in[corners[1], :, lanes]), below)
            return weight[0][tap] * above + weight[1][tap] * middle + weight[2][tap] * below

        low, high = edge(left, 0, (0, 2)), edge(right, 2, (1, 3))
        window = {}
        for r in out_rows:
            window = {a: window[a] if a in window else fetch(a) for a in (r - 1, r, r + 1)}
            before, now, after = window[r - 1], window[r], window[r + 1]
            taps = [
                [weight[0][b] * before[g] + weight[1][b] * now[g] + weight[2][b] * after[g] for g in range(groups)]
                for b in range(3)
            ]
            from_low = [wide(low[r : r + 1])] + [pltpu.roll(v, 1, axis=0) for v in taps[0]]
            from_high = [pltpu.roll(v, 7, axis=0) for v in taps[2]] + [wide(high[r : r + 1])]
            yield [
                (taps[1][g] + bias)
                + jnp.where(sub == 0, from_low[g], from_low[g + 1])
                + jnp.where(sub == 7, from_high[g + 1], from_high[g])
                for g in range(groups)
            ]

    def gate_tile(lanes, width, out_rows, carry):
        at = 0
        for sums_of_row in conv(lanes, width, out_rows):
            for v in sums_of_row:
                half = 0.5 * v
                v = half + half * jnp.tanh(half)
                if width < LANES:
                    v = jnp.concatenate([v, jnp.zeros((8, LANES - width), F32)], axis=1)
                v = pltpu.roll(v, GATE_SHIFT, axis=1)
                gates[at] = jnp.where(lane < GATE_SHIFT, carry[at], v)
                carry[at] = v
                at += 1

    def value_tile(lanes, width, out_rows):
        at = 0
        for r, sums_of_row in zip(out_rows, conv(lanes, LANES, out_rows)):
            for g in range(0, groups, 2):
                out = jnp.concatenate(
                    [sums_of_row[g] * gates[at], sums_of_row[g + 1] * gates[at + 1]], axis=0
                ).astype(BF16)
                if width == LANES:
                    gbuf[r, 8 * g : 8 * g + 16, lanes] = out
                else:
                    gbuf[r, 8 * g : 8 * g + 16, HID - width : HID] = out[:, :width]
                at += 2

    def tile_at(t):
        return pl.ds(pl.multiple_of(t * LANES, LANES), LANES)

    def first_tile(out_rows, carry):
        for at in range(len(out_rows) * groups):
            carry[at] = jnp.zeros((8, LANES), F32)
        gate_tile(slice(GATE_TILE * LANES, GATE_TILE * LANES + LANES), LANES, out_rows, carry)

    def some_tiles(out_rows, carry, begin, end):
        @pl.loop(begin, end)
        def _(u):
            gate_tile(tile_at(u + GATE_TILE + 1), LANES, out_rows, carry)
            value_tile(tile_at(u), LANES, out_rows)

    def last_tile(out_rows, carry):
        gate_tile(slice(full_tiles * LANES, channels), tail, out_rows, carry)
        value_tile(slice(GATE_TILE * LANES, GATE_TILE * LANES + LANES), HID % LANES, out_rows)

    loads[3].wait()
    loads[4].wait()
    sum_x()
    advance(2)
    advance(3)
    pl.when(has_right)(to_left.wait_recv)
    pl.when(has_left)(to_right.wait_recv)
    inner = list(range(1, rows - 1))
    steps = [(sum_y, 4, 5), (sum_z, 6, 7), (share_y, 8, 9), (share_x, 10)]
    first_tile(inner, prev)

    @pl.loop(0, GATE_TILE)
    def _(u):
        for at, (step, *chunks) in zip(STEP_AT, steps):
            @pl.when(u == at)
            def _():
                step()
                for next_chunk in chunks:
                    advance(next_chunk)

        gate_tile(tile_at(u + GATE_TILE + 1), LANES, inner, prev)
        value_tile(tile_at(u), LANES, inner)

    last_tile(inner, prev)
    store_inner = pltpu.make_async_copy(
        gbuf.at[pl.ds(1, rows - 2)], gated_hbm.at[pl.ds(1, rows - 2)], store_sem.at[0]
    )
    store_inner.start()

    received_chunk(CHUNKS - 1)
    mate_row.wait_recv()

    @pl.when(crosses)
    def _():
        far_tail.wait_recv()
        halo[core, :, full_tiles * LANES :] = tail_in[:, :tail]

    for i, there, _, _ in diagonals:
        pl.when(there)(to_corner[3 - i].wait_recv)
    outer = [0, rows - 1]
    first_tile(outer, prev)

    @pl.loop(0, CHUNKS - 1)
    def _(at):
        received_chunk(at)
        some_tiles(outer, prev, at * CHUNK, at * CHUNK + CHUNK)

    some_tiles(outer, prev, (CHUNKS - 1) * CHUNK, GATE_TILE)
    last_tile(outer, prev)
    store_first = pltpu.make_async_copy(gbuf.at[0], gated_hbm.at[0], store_sem.at[2])
    store_last = pltpu.make_async_copy(gbuf.at[rows - 1], gated_hbm.at[rows - 1], store_sem.at[3])
    store_first.start()
    store_last.start()
    get_core.wait_recv()
    store_state = pltpu.make_async_copy(total, state_hbm, store_sem.at[1])
    store_state.start()

    for step in range(CHUNKS, CHUNKS + DEPTH):
        advance(step)
    mate_row.wait_send()
    pl.when(crosses)(far_tail.wait_send)
    pl.when(has_left)(to_left.wait_send)
    pl.when(has_right)(to_right.wait_send)
    for i, there, _, _ in diagonals:
        pl.when(there)(to_corner[i].wait_send)
    for copy in [add_core, give_core] + add_x + add_y + add_z + give_y + give_x:
        copy.wait_send()
    for store in [store_inner, store_state, store_first, store_last]:
        store.wait()


def mix(keys, values, features, conv_weight, conv_bias):
    rows, cols, channels = features.shape
    width = keys.shape[2]
    sem = pltpu.SemaphoreType.DMA
    tiles = lambda *lead: pltpu.VMEM(lead + (8, LANES), F32)
    anywhere = pl.BlockSpec(memory_space=pl.ANY)
    return pl.pallas_call(
        mix_kernel,
        name="mix",
        out_shape=(
            jax.ShapeDtypeStruct((TILES, 8, LANES), F32),
            jax.ShapeDtypeStruct((rows, cols, HID), BF16),
        ),
        in_specs=[pl.BlockSpec(memory_space=pltpu.HBM)] * 5,
        out_specs=[anywhere] * 2,
        scratch_shapes=[
            pltpu.VMEM((rows, cols, width), BF16),
            pltpu.VMEM((rows, cols, width), BF16),
            pltpu.VMEM((rows, cols, channels), BF16),
            pltpu.VMEM((3, 3, channels), BF16),
            pltpu.VMEM((1, channels), BF16),
            pltpu.VMEM((rows, cols, HID), BF16),
            pltpu.VMEM((2, cols, channels), BF16),
            pltpu.VMEM((rows, channels), BF16),
            pltpu.VMEM((rows, channels), BF16),
            pltpu.VMEM((rows, channels), BF16),
            pltpu.VMEM((rows, channels), BF16),
            pltpu.VMEM((4, 1, channels), F32),
            pltpu.VMEM((4, 1, channels), F32),
            pltpu.VMEM((cols, LANES), BF16),
            pltpu.VMEM((cols, LANES), BF16),
            tiles((rows - 2) * cols // 8),
            tiles((rows - 2) * cols // 8),
            tiles(TILES),
            tiles(HALF),
            tiles(3, USED),
            tiles(7, SHARE),
            tiles(3, SHARE),
            tiles(TILES),
            sem((5,)), sem((4,)), sem((2, CHUNKS)), sem((2, CHUNKS)), sem((2,)), sem((2,)),
            sem((2,)), sem((2,)), sem((4,)), sem((4,)),
            sem((2,)), sem((2,)), sem((6,)), sem((6,)), sem((7,)), sem((7,)), sem((6,)), sem((6,)),
        ],
        compiler_params=pltpu.CompilerParams(
            collective_id=0, has_side_effects=True, vmem_limit_bytes=48 << 20
        ),
        cost_estimate=pl.CostEstimate(flops=100_000_000, bytes_accessed=12_000_000, transcendentals=1_500_000),
    )(keys, values, features, conv_weight, conv_bias.reshape(1, channels))


def attend_kernel(q_hbm, state, mixed_hbm, attended_hbm, gated_hbm, qbuf, abuf, matrix, sem):
    rows, cols, width = qbuf.shape
    move = pltpu.make_async_copy(mixed_hbm, gated_hbm, sem.at[0])
    load = pltpu.make_async_copy(q_hbm, qbuf, sem.at[1])
    load.start()
    move.start()

    lane = iota((HEAD_DIM, LANES), 1)
    head_of_lane = lax.div(lane, HEAD_DIM)

    def split(v):
        high = v.astype(BF16)
        return high, (v - high.astype(F32)).astype(BF16)

    def rows_of(block):
        return jnp.concatenate([state[slot(block * 4 + group)] for group in range(4)], axis=0)

    sum_high, sum_low = split(rows_of(BLOCKS))

    def block_diagonal(v):
        v = v.astype(F32)
        return jnp.concatenate([jnp.where(head_of_lane == h, v, 0.0) for h in range(4)], axis=0).astype(BF16)

    def build(block):
        high, low = split(rows_of(block))
        picks = (iota((LANES, LANES), 0) == block * 4 + lax.div(iota((LANES, LANES), 1), HEAD_DIM))
        picks = picks.astype(F32).astype(BF16)
        key_high = jnp.dot(sum_high, picks, preferred_element_type=F32)
        key_low = jnp.dot(sum_low, picks, preferred_element_type=F32)
        top = jnp.concatenate([block_diagonal(high), block_diagonal(key_high)], axis=1)
        bottom = jnp.concatenate([block_diagonal(low), block_diagonal(key_low)], axis=1)
        matrix[block] = jnp.concatenate([top, bottom], axis=0)

    for block in range(BLOCKS):
        build(block)
    load.wait()
    for block in range(BLOCKS):
        start = block * LANES
        size = min(LANES, width - start)
        queries = jnp.maximum(qbuf[:, :, start : start + size], 0).reshape(rows * cols, size)
        if size < LANES:
            queries = jnp.concatenate([queries, jnp.zeros((rows * cols, LANES - size), BF16)], axis=1)
        both = jnp.dot(jnp.concatenate([queries, queries], axis=1), matrix[block], preferred_element_type=F32)
        out = (both[:, :LANES] / (both[:, LANES:] + 1e-15)).astype(BF16).reshape(rows, cols, LANES)
        abuf[:, :, start : start + size] = out[:, :, :size]
    store = pltpu.make_async_copy(abuf, attended_hbm, sem.at[2])
    store.start()
    store.wait()
    move.wait()


def attend(queries, state, mixed):
    anywhere = pl.BlockSpec(memory_space=pl.ANY)
    return pl.pallas_call(
        attend_kernel,
        name="attend",
        out_shape=(
            jax.ShapeDtypeStruct(queries.shape, BF16),
            jax.ShapeDtypeStruct(mixed.shape, BF16),
        ),
        in_specs=[anywhere, pl.BlockSpec(memory_space=pltpu.VMEM), anywhere],
        out_specs=[anywhere] * 2,
        scratch_shapes=[
            pltpu.VMEM(queries.shape, BF16),
            pltpu.VMEM(queries.shape, BF16),
            pltpu.VMEM((BLOCKS, 2 * LANES, 2 * LANES), BF16),
            pltpu.SemaphoreType.DMA((3,)),
        ],
        compiler_params=pltpu.CompilerParams(vmem_limit_bytes=32 << 20),
        cost_estimate=pl.CostEstimate(flops=600_000_000, bytes_accessed=8_000_000, transcendentals=0),
    )(queries, state, mixed)


def on_device(queries, keys, values, features, conv_weight, conv_bias):
    hold = functools.partial(pltpu.with_memory_space_constraint, memory_space=pltpu.HBM)
    keys, values, conv_weight = hold(keys), hold(values), hold(conv_weight)
    state, mixed = mix(keys, values, features, conv_weight, conv_bias)
    return attend(queries, state, mixed)


def solution(mesh):
    return jax.shard_map(
        on_device,
        mesh=mesh,
        in_specs=(
            P("row", "col", None),
            P("row", "col", None),
            P("row", "col", None),
            P("row", "col", None),
            P(),
            P(),
        ),
        out_specs=(P("row", "col", None), P("row", "col", None)),
        check_vma=False,
    )
```

time: 378 us -> 50.4 us (0.13)
  the two profiles are of different devices: /device:TPU:1 before, /device:TPU:2 now
where the time goes in v2:
time: 50.4 us; the launch traced here: 50.2 us
  Pallas kernels  48.8 us (97%)
  local copies, waits for them, and re-layouts  0.77 us (2%)
  between operations  0.66 us (1%)
    pallas_call x1, Pallas kernels, mix(): pl.pallas_call(mix_kernel, name='mix', out_shape=(jax.ShapeDtypeStruct((T...  46.5 us
    pallas_call x1, Pallas kernels, attend(): pl.pallas_call(attend_kernel, name='attend', out_shape=(jax.ShapeDtypeStr...  2.32 us

profile of v2, /device:TPU:2, one launch (start us, length us, event | category | flops | bytes accessed | tf_op | source)
XLA Modules:
  0.0 50.2 jit_solution(2153836318368740391)
XLA Ops:
  0.6 0.8 %reshape.7.b_hbm = bf16[1,11200]{1,0:T(2,128)(2,1)S(1)} reshape(bf16[11200]{0:T(1024)(128)(2,1)} %param.11) | data formatting | bytes 44800 | tf_op jit(solution)/shard_map/reshape | solution.py:534
  1.4 0.0 copy-start
  1.4 46.5 %mix.1 = (f32[96,8,128]{2,1,0:T(8,128)S(1)}, bf16[8,32,5600]{2,1,0:T(8,128)(2,1)S(1)}) custom-call(bf16[8,32,2240]{2,1,0:T(8,128)(2,1)} %k_hbm.1, bf16[8,32,2240]{2,1,0:T(8,128)(2,1)} %v_hbm.1, bf16[8,32,11200]{2,1,0:T(8,128)(2,1)} %x_hbm.1, bf16[3,3,11200]{2,1,0:T(4,128)(2,1)} %w_hbm.1, bf16[1,11200]{1,0:T(2,128)(2,1)S(1)} %reshape.7.b_hbm), custom_call_target="tpu_custom_call" | custom-call | flops 100000000 | bytes 12000000 | tf_op jit(solution)/shard_map/mix/pallas_call | solution.py:493
  47.9 0.0 copy-done
  47.9 2.3 %attend.1 = (bf16[8,32,2240]{2,1,0:T(8,128)(2,1)}, bf16[8,32,5600]{2,1,0:T(8,128)(2,1)}) custom-call(bf16[8,32,2240]{2,1,0:T(8,128)(2,1)S(1)} %copy-done, f32[96,8,128]{2,1,0:T(8,128)S(1)} %get-tuple-element.4.state, bf16[8,32,5600]{2,1,0:T(8,128)(2,1)S(1)} %get-tuple-element.5.mixed_hbm), custom_call_target="tpu_custom_call" | custom-call | flops 600000000 | bytes 8000000 | tf_op jit(solution)/shard_map/attend/pallas_call | solution.py:590
Async XLA Ops:
  1.4 46.5 %copy-start = (bf16[8,32,2240]{2,1,0:T(8,128)(2,1)S(1)}, bf16[8,32,2240]{2,1,0:T(8,128)(2,1)}, u32[]{:S(2)}) copy-start(bf16[8,32,2240]{2,1,0:T(8,128)(2,1)} %q_hbm.1) | copy-start | bytes 3440644

commit v3 on v2

--- a/solution.py
+++ b/solution.py
@@ -24,8 +24,9 @@
 GATE_SHIFT = LANES - HID % LANES
 CHUNK = 4
 CHUNKS = 11
-DEPTH = 2
-STEP_AT = (4, 18, 28, 41)
+FIRST, SECOND = 3,6
+SUM_X_AT, SUM_Y_AT, SUM_Z_AT = 24, 42, 30
+SHARE_X_AT = 4
 
 
 def slot(tile):
@@ -161,14 +162,13 @@
             for copy in chunk(at):
                 copy.wait_recv()
 
-    def advance(step):
-        if step >= DEPTH:
-            sent_chunk(order[step - DEPTH])
-        if step < CHUNKS:
+    order = [CHUNKS - 1] + list(range(CHUNKS - 1))
+
+    def start_chunks(begin, end):
+        for step in range(begin, end):
             start_chunk(order[step])
 
-    order = [CHUNKS - 1] + list(range(CHUNKS - 1))
-    advance(0)
+    start_chunks(0, FIRST)
 
     lane = iota((8, LANES), 1)
 
@@ -316,11 +316,10 @@
         return bbuf[:, lanes].astype(F32)
 
     pl.when(crosses)(far_tail.start)
-    advance(1)
 
     groups = cols // 8
 
-    def conv(lanes, width, out_rows):
+    def conv(lanes, width, out_rows, out_groups):
         sub = iota((8, width), 0)
 
         def wide(v):
@@ -351,92 +350,91 @@
                 below = jnp.where(sub == 7, wide(corner_in[corners[1], :, lanes]), below)
             return weight[0][tap] * above + weight[1][tap] * middle + weight[2][tap] * below
 
-        low, high = edge(left, 0, (0, 2)), edge(right, 2, (1, 3))
+        if 0 in out_groups:
+            low, high = edge(left, 0, (0, 2)), edge(right, 2, (1, 3))
         window = {}
         for r in out_rows:
             window = {a: window[a] if a in window else fetch(a) for a in (r - 1, r, r + 1)}
             before, now, after = window[r - 1], window[r], window[r + 1]
-            taps = [
-                [weight[0][b] * before[g] + weight[1][b] * now[g] + weight[2][b] * after[g] for g in range(groups)]
-                for b in range(3)
+
+            def tap(b, g):
+                return weight[0][b] * before[g] + weight[1][b] * now[g] + weight[2][b] * after[g]
+
+            from_low, from_high = {}, {}
+            for g in range(groups):
+                if g in out_groups or g + 1 in out_groups:
+                    from_low[g] = pltpu.roll(tap(0, g), 1, axis=0)
+                if g in out_groups or g - 1 in out_groups:
+                    from_high[g] = pltpu.roll(tap(2, g), 7, axis=0)
+            if 0 in out_groups:
+                from_low[-1], from_high[groups] = wide(low[r : r + 1]), wide(high[r : r + 1])
+            yield [
+                (tap(1, g) + bias)
+                + jnp.where(sub == 0, from_low[g - 1], from_low[g])
+                + jnp.where(sub == 7, from_high[g + 1], from_high[g])
+                for g in out_groups
             ]
-            from_low = [wide(low[r : r + 1])] + [pltpu.roll(v, 1, axis=0) for v in taps[0]]
-            from_high = [pltpu.roll(v, 7, axis=0) for v in taps[2]] + [wide(high[r : r + 1])]
-            yield [
-                (taps[1][g] + bias)
-                + jnp.where(sub == 0, from_low[g], from_low[g + 1])
-                + jnp.where(sub == 7, from_high[g + 1], from_high[g])
-                for g in range(groups)
-            ]
-
-    def gate_tile(lanes, width, out_rows, carry):
+
+    def gate_tile(lanes, width, where):
         at = 0
-        for sums_of_row in conv(lanes, width, out_rows):
+        for sums_of_row in conv(lanes, width, *where):
             for v in sums_of_row:
                 half = 0.5 * v
                 v = half + half * jnp.tanh(half)
                 if width < LANES:
                     v = jnp.concatenate([v, jnp.zeros((8, LANES - width), F32)], axis=1)
                 v = pltpu.roll(v, GATE_SHIFT, axis=1)
-                gates[at] = jnp.where(lane < GATE_SHIFT, carry[at], v)
-                carry[at] = v
+                gates[at] = jnp.where(lane < GATE_SHIFT, prev[at], v)
+                prev[at] = v
                 at += 1
 
-    def value_tile(lanes, width, out_rows):
+    def value_tile(lanes, width, where):
         at = 0
-        for r, sums_of_row in zip(out_rows, conv(lanes, LANES, out_rows)):
-            for g in range(0, groups, 2):
-                out = jnp.concatenate(
-                    [sums_of_row[g] * gates[at], sums_of_row[g + 1] * gates[at + 1]], axis=0
-                ).astype(BF16)
+        for r, sums_of_row in zip(where[0], conv(lanes, LANES, *where)):
+            for g, v in zip(where[1], sums_of_row):
+                out = (v * gates[at]).astype(BF16)
                 if width == LANES:
-                    gbuf[r, 8 * g : 8 * g + 16, lanes] = out
+                    gbuf[r, 8 * g : 8 * g + 8, lanes] = out
                 else:
-                    gbuf[r, 8 * g : 8 * g + 16, HID - width : HID] = out[:, :width]
-                at += 2
+                    gbuf[r, 8 * g : 8 * g + 8, HID - width : HID] = out[:, :width]
+                at += 1
 
     def tile_at(t):
         return pl.ds(pl.multiple_of(t * LANES, LANES), LANES)
 
-    def first_tile(out_rows, carry):
-        for at in range(len(out_rows) * groups):
-            carry[at] = jnp.zeros((8, LANES), F32)
-        gate_tile(slice(GATE_TILE * LANES, GATE_TILE * LANES + LANES), LANES, out_rows, carry)
-
-    def some_tiles(out_rows, carry, begin, end):
+    def first_tile(where):
+        for at in range(len(where[0]) * len(where[1])):
+            prev[at] = jnp.zeros((8, LANES), F32)
+        gate_tile(slice(GATE_TILE * LANES, GATE_TILE * LANES + LANES), LANES, where)
+
+    def some_tiles(where, begin, end, actions=()):
         @pl.loop(begin, end)
         def _(u):
-            gate_tile(tile_at(u + GATE_TILE + 1), LANES, out_rows, carry)
-            value_tile(tile_at(u), LANES, out_rows)
-
-    def last_tile(out_rows, carry):
-        gate_tile(slice(full_tiles * LANES, channels), tail, out_rows, carry)
-        value_tile(slice(GATE_TILE * LANES, GATE_TILE * LANES + LANES), HID % LANES, out_rows)
+            for at, action, argument in actions:
+                pl.when(u == at)(functools.partial(action, *argument))
+            gate_tile(tile_at(u + GATE_TILE + 1), LANES, where)
+            value_tile(tile_at(u), LANES, where)
+
+    def last_tile(where):
+        gate_tile(slice(full_tiles * LANES, channels), tail, where)
+        value_tile(slice(GATE_TILE * LANES, GATE_TILE * LANES + LANES), HID % LANES, where)
 
     loads[3].wait()
     loads[4].wait()
-    sum_x()
-    advance(2)
-    advance(3)
+    where = (list(range(1, rows - 1)), list(range(1, groups - 1)))
+    first_tile(where)
+    some_tiles(where, 0, GATE_TILE, [
+        (SUM_X_AT, sum_x, ()), (SUM_Y_AT, sum_y, ()), (SUM_Y_AT, start_chunks, (FIRST, SECOND)),
+    ])
+    last_tile(where)
+
     pl.when(has_right)(to_left.wait_recv)
     pl.when(has_left)(to_right.wait_recv)
-    inner = list(range(1, rows - 1))
-    steps = [(sum_y, 4, 5), (sum_z, 6, 7), (share_y, 8, 9), (share_x, 10)]
-    first_tile(inner, prev)
-
-    @pl.loop(0, GATE_TILE)
-    def _(u):
-        for at, (step, *chunks) in zip(STEP_AT, steps):
-            @pl.when(u == at)
-            def _():
-                step()
-                for next_chunk in chunks:
-                    advance(next_chunk)
-
-        gate_tile(tile_at(u + GATE_TILE + 1), LANES, inner, prev)
-        value_tile(tile_at(u), LANES, inner)
-
-    last_tile(inner, prev)
+    where = (list(range(1, rows - 1)), [0, groups - 1])
+    first_tile(where)
+    some_tiles(where, 0, GATE_TILE, [(SUM_Z_AT, sum_z, ()), (SUM_Z_AT, start_chunks, (SECOND, CHUNKS))])
+    last_tile(where)
+    share_y()
     store_inner = pltpu.make_async_copy(
         gbuf.at[pl.ds(1, rows - 2)], gated_hbm.at[pl.ds(1, rows - 2)], store_sem.at[0]
     )
@@ -452,16 +450,17 @@
 
     for i, there, _, _ in diagonals:
         pl.when(there)(to_corner[3 - i].wait_recv)
-    outer = [0, rows - 1]
-    first_tile(outer, prev)
+    where = ([0, rows - 1], list(range(groups)))
+    first_tile(where)
 
     @pl.loop(0, CHUNKS - 1)
     def _(at):
+        pl.when(at == SHARE_X_AT)(share_x)
         received_chunk(at)
-        some_tiles(outer, prev, at * CHUNK, at * CHUNK + CHUNK)
-
-    some_tiles(outer, prev, (CHUNKS - 1) * CHUNK, GATE_TILE)
-    last_tile(outer, prev)
+        some_tiles(where, at * CHUNK, at * CHUNK + CHUNK)
+
+    some_tiles(where, (CHUNKS - 1) * CHUNK, GATE_TILE)
+    last_tile(where)
     store_first = pltpu.make_async_copy(gbuf.at[0], gated_hbm.at[0], store_sem.at[2])
     store_last = pltpu.make_async_copy(gbuf.at[rows - 1], gated_hbm.at[rows - 1], store_sem.at[3])
     store_first.start()
@@ -470,8 +469,8 @@
     store_state = pltpu.make_async_copy(total, state_hbm, store_sem.at[1])
     store_state.start()
 
-    for step in range(CHUNKS, CHUNKS + DEPTH):
-        advance(step)
+    for at in order:
+        sent_chunk(at)
     mate_row.wait_send()
     pl.when(crosses)(far_tail.wait_send)
     pl.when(has_left)(to_left.wait_send)

time: 50.4 us -> 46.2 us (0.917)
  the two profiles are of different devices: /device:TPU:2 before, /device:TPU:68 now
where the time goes in v3:
time: 46.2 us; the launch traced here: 46.1 us
  Pallas kernels  44.7 us (97%)
  local copies, waits for them, and re-layouts  0.77 us (2%)
  between operations  0.66 us (1%)
    pallas_call x1, Pallas kernels, mix(): pl.pallas_call(mix_kernel, name='mix', out_shape=(jax.ShapeDtypeStruct((T...  42.3 us
    pallas_call x1, Pallas kernels, attend(): pl.pallas_call(attend_kernel, name='attend', out_shape=(jax.ShapeDtypeStr...  2.32 us

profile of v3, /device:TPU:68, one launch (start us, length us, event | category | flops | bytes accessed | tf_op | source)
XLA Modules:
  0.0 46.1 jit_solution(5380526671208614856)
XLA Ops:
  0.6 0.8 %reshape.7.b_hbm = bf16[1,11200]{1,0:T(2,128)(2,1)S(1)} reshape(bf16[11200]{0:T(1024)(128)(2,1)} %param.11) | data formatting | bytes 44800 | tf_op jit(solution)/shard_map/reshape | solution.py:533
  1.4 0.0 copy-start
  1.4 42.3 %mix.1 = (f32[96,8,128]{2,1,0:T(8,128)S(1)}, bf16[8,32,5600]{2,1,0:T(8,128)(2,1)S(1)}) custom-call(bf16[8,32,2240]{2,1,0:T(8,128)(2,1)} %k_hbm.1, bf16[8,32,2240]{2,1,0:T(8,128)(2,1)} %v_hbm.1, bf16[8,32,11200]{2,1,0:T(8,128)(2,1)} %x_hbm.1, bf16[3,3,11200]{2,1,0:T(4,128)(2,1)} %w_hbm.1, bf16[1,11200]{1,0:T(2,128)(2,1)S(1)} %reshape.7.b_hbm), custom_call_target="tpu_custom_call" | custom-call | flops 100000000 | bytes 12000000 | tf_op jit(solution)/shard_map/mix/pallas_call | solution.py:492
  43.8 0.0 copy-done
  43.8 2.3 %attend.1 = (bf16[8,32,2240]{2,1,0:T(8,128)(2,1)}, bf16[8,32,5600]{2,1,0:T(8,128)(2,1)}) custom-call(bf16[8,32,2240]{2,1,0:T(8,128)(2,1)S(1)} %copy-done, f32[96,8,128]{2,1,0:T(8,128)S(1)} %get-tuple-element.4.state, bf16[8,32,5600]{2,1,0:T(8,128)(2,1)S(1)} %get-tuple-element.5.mixed_hbm), custom_call_target="tpu_custom_call" | custom-call | flops 600000000 | bytes 8000000 | tf_op jit(solution)/shard_map/attend/pallas_call | solution.py:589
Async XLA Ops:
  1.4 42.4 %copy-start = (bf16[8,32,2240]{2,1,0:T(8,128)(2,1)S(1)}, bf16[8,32,2240]{2,1,0:T(8,128)(2,1)}, u32[]{:S(2)}) copy-start(bf16[8,32,2240]{2,1,0:T(8,128)(2,1)} %q_hbm.1) | copy-start | bytes 3440644

commit v4 on v3

--- a/solution.py
+++ b/solution.py
@@ -24,8 +24,8 @@
 GATE_SHIFT = LANES - HID % LANES
 CHUNK = 4
 CHUNKS = 11
-FIRST, SECOND = 3,6
-SUM_X_AT, SUM_Y_AT, SUM_Z_AT = 24, 42, 30
+FIRST, SECOND = 3, 6
+SUM_X_AT, SUM_Y_AT, SUM_Z_AT = 24, 40, 28
 SHARE_X_AT = 4
 
 
@@ -51,7 +51,7 @@
 def mix_kernel(
     k_hbm, v_hbm, x_hbm, w_hbm, b_hbm,
     state_hbm, gated_hbm,
-    kbuf, vbuf, xbuf, wbuf, bbuf, gbuf,
+    kbuf, vbuf, xbuf, wbuf, bbuf, bias_row, gbuf,
     halo, left, right, send_left, send_right,
     corner_in, corner_out, tail_in, tail_out, prev, gates,
     part, recv_core, recv_x, recv_z, recv_y, total,
@@ -309,11 +309,13 @@
         remote(corner_out.at[i], corner_in.at[3 - i], corner_send.at[i], corner_recv.at[3 - i], (row + a, col + b))
         for i, _, a, b in diagonals
     ]
-    for i, there, _, _ in diagonals:
-        pl.when(there)(to_corner[i].start)
+    def send_corners():
+        for i, there, _, _ in diagonals:
+            pl.when(there)(to_corner[i].start)
+
 
     def bias_at(lanes, width):
-        return bbuf[:, lanes].astype(F32)
+        return bias_row[:, lanes]
 
     pl.when(crosses)(far_tail.start)
 
@@ -375,7 +377,7 @@
                 for g in out_groups
             ]
 
-    def gate_tile(lanes, width, where):
+    def gate_tile(lanes, width, where, second=0):
         at = 0
         for sums_of_row in conv(lanes, width, *where):
             for v in sums_of_row:
@@ -384,15 +386,15 @@
                 if width < LANES:
                     v = jnp.concatenate([v, jnp.zeros((8, LANES - width), F32)], axis=1)
                 v = pltpu.roll(v, GATE_SHIFT, axis=1)
-                gates[at] = jnp.where(lane < GATE_SHIFT, prev[at], v)
+                gates[second + at] = jnp.where(lane < GATE_SHIFT, prev[at], v)
                 prev[at] = v
                 at += 1
 
-    def value_tile(lanes, width, where):
+    def value_tile(lanes, width, where, second=0):
         at = 0
         for r, sums_of_row in zip(where[0], conv(lanes, LANES, *where)):
             for g, v in zip(where[1], sums_of_row):
-                out = (v * gates[at]).astype(BF16)
+                out = (v * gates[second + at]).astype(BF16)
                 if width == LANES:
                     gbuf[r, 8 * g : 8 * g + 8, lanes] = out
                 else:
@@ -407,13 +409,22 @@
             prev[at] = jnp.zeros((8, LANES), F32)
         gate_tile(slice(GATE_TILE * LANES, GATE_TILE * LANES + LANES), LANES, where)
 
-    def some_tiles(where, begin, end, actions=()):
-        @pl.loop(begin, end)
-        def _(u):
+    def some_tiles(where, begin, count, actions=()):
+        def one(u, second=0):
+            gate_tile(tile_at(u + GATE_TILE + 1), LANES, where, second)
+            value_tile(tile_at(u), LANES, where, second)
+
+        pairs = count // 2
+
+        @pl.loop(0, pairs)
+        def _(pair):
             for at, action, argument in actions:
-                pl.when(u == at)(functools.partial(action, *argument))
-            gate_tile(tile_at(u + GATE_TILE + 1), LANES, where)
-            value_tile(tile_at(u), LANES, where)
+                pl.when(pair == at // 2)(functools.partial(action, *argument))
+            one(begin + 2 * pair)
+            one(begin + 2 * pair + 1, len(where[0]) * len(where[1]))
+
+        if count % 2:
+            one(begin + count - 1)
 
     def last_tile(where):
         gate_tile(slice(full_tiles * LANES, channels), tail, where)
@@ -421,10 +432,13 @@
 
     loads[3].wait()
     loads[4].wait()
+    for at in range(0, channels, 1024):
+        piece = bbuf[at : min(at + 1024, channels)].astype(F32)
+        bias_row[:, at : min(at + 1024, channels)] = piece.reshape(1, -1)
     where = (list(range(1, rows - 1)), list(range(1, groups - 1)))
     first_tile(where)
     some_tiles(where, 0, GATE_TILE, [
-        (SUM_X_AT, sum_x, ()), (SUM_Y_AT, sum_y, ()), (SUM_Y_AT, start_chunks, (FIRST, SECOND)),
+        (SUM_X_AT, sum_x, ()), (SUM_Y_AT, sum_y, ()), (SUM_Y_AT, send_corners, ()), (SUM_Y_AT, start_chunks, (FIRST, SECOND)),
     ])
     last_tile(where)
 
@@ -457,9 +471,9 @@
     def _(at):
         pl.when(at == SHARE_X_AT)(share_x)
         received_chunk(at)
-        some_tiles(where, at * CHUNK, at * CHUNK + CHUNK)
-
-    some_tiles(where, (CHUNKS - 1) * CHUNK, GATE_TILE)
+        some_tiles(where, at * CHUNK, CHUNK)
+
+    some_tiles(where, (CHUNKS - 1) * CHUNK, GATE_TILE - (CHUNKS - 1) * CHUNK)
     last_tile(where)
     store_first = pltpu.make_async_copy(gbuf.at[0], gated_hbm.at[0], store_sem.at[2])
     store_last = pltpu.make_async_copy(gbuf.at[rows - 1], gated_hbm.at[rows - 1], store_sem.at[3])
@@ -503,7 +517,8 @@
             pltpu.VMEM((rows, cols, width), BF16),
             pltpu.VMEM((rows, cols, channels), BF16),
             pltpu.VMEM((3, 3, channels), BF16),
-            pltpu.VMEM((1, channels), BF16),
+            pltpu.VMEM((channels,), BF16),
+            pltpu.VMEM((1, channels), F32),
             pltpu.VMEM((rows, cols, HID), BF16),
             pltpu.VMEM((2, cols, channels), BF16),
             pltpu.VMEM((rows, channels), BF16),
@@ -530,7 +545,7 @@
             collective_id=0, has_side_effects=True, vmem_limit_bytes=48 << 20
         ),
         cost_estimate=pl.CostEstimate(flops=100_000_000, bytes_accessed=12_000_000, transcendentals=1_500_000),
-    )(keys, values, features, conv_weight, conv_bias.reshape(1, channels))
+    )(keys, values, features, conv_weight, conv_bias)
 
 
 def attend_kernel(q_hbm, state, mixed_hbm, attended_hbm, gated_hbm, qbuf, abuf, matrix, sem):

time: 46.2 us -> 45.1 us (0.976)
  the two profiles are of different devices: /device:TPU:68 before, /device:TPU:1 now
where the time goes in v4:
time: 45.1 us; the launch traced here: 44.7 us
  Pallas kernels  43.3 us (96%)
  local copies, waits for them, and re-layouts  0.73 us (2%)
  between operations  0.66 us (1%)
    pallas_call x1, Pallas kernels, mix(): pl.pallas_call(mix_kernel, name='mix', out_shape=(jax.ShapeDtypeStruct((T...  41 us
    pallas_call x1, Pallas kernels, attend(): pl.pallas_call(attend_kernel, name='attend', out_shape=(jax.ShapeDtypeStr...  2.32 us

profile of v4, /device:TPU:1, one launch (start us, length us, event | category | flops | bytes accessed | tf_op | source)
XLA Modules:
  0.0 44.7 jit_solution(13558291390048989896)
XLA Ops:
  0.6 0.0 copy-start.1
  0.6 0.7 %copy-done.1 = bf16[11200]{0:T(1024)(128)(2,1)S(1)} copy-done((bf16[11200]{0:T(1024)(128)(2,1)S(1)}, bf16[11200]{0:T(1024)(128)(2,1)}, u32[]{:S(2)}) %copy-start.1) | copy-done | bytes 22424
  1.4 0.0 copy-start
  1.4 41.0 %mix.1 = (f32[96,8,128]{2,1,0:T(8,128)S(1)}, bf16[8,32,5600]{2,1,0:T(8,128)(2,1)S(1)}) custom-call(bf16[8,32,2240]{2,1,0:T(8,128)(2,1)} %k_hbm.1, bf16[8,32,2240]{2,1,0:T(8,128)(2,1)} %v_hbm.1, bf16[8,32,11200]{2,1,0:T(8,128)(2,1)} %x_hbm.1, bf16[3,3,11200]{2,1,0:T(4,128)(2,1)} %w_hbm.1, bf16[11200]{0:T(1024)(128)(2,1)S(1)} %copy-done.1), custom_call_target="tpu_custom_call" | custom-call | flops 100000000 | bytes 12000000 | tf_op jit(solution)/shard_map/mix/pallas_call | solution.py:506
  42.4 0.0 copy-done
  42.4 2.3 %attend.1 = (bf16[8,32,2240]{2,1,0:T(8,128)(2,1)}, bf16[8,32,5600]{2,1,0:T(8,128)(2,1)}) custom-call(bf16[8,32,2240]{2,1,0:T(8,128)(2,1)S(1)} %copy-done, f32[96,8,128]{2,1,0:T(8,128)S(1)} %get-tuple-element.4.state, bf16[8,32,5600]{2,1,0:T(8,128)(2,1)S(1)} %get-tuple-element.5.mixed_hbm), custom_call_target="tpu_custom_call" | custom-call | flops 600000000 | bytes 8000000 | tf_op jit(solution)/shard_map/attend/pallas_call | solution.py:604
Async XLA Ops:
  0.6 0.7 %copy-start.1 = (bf16[11200]{0:T(1024)(128)(2,1)S(1)}, bf16[11200]{0:T(1024)(128)(2,1)}, u32[]{:S(2)}) copy-start(bf16[11200]{0:T(1024)(128)(2,1)} %b_hbm.1) | copy-start | bytes 67204
  1.4 41.0 %copy-start = (bf16[8,32,2240]{2,1,0:T(8,128)(2,1)S(1)}, bf16[8,32,2240]{2,1,0:T(8,128)(2,1)}, u32[]{:S(2)}) copy-start(bf16[8,32,2240]{2,1,0:T(8,128)(2,1)} %q_hbm.1) | copy-start | bytes 3440644
